TPU v7x, 256 devices: a whole 4x4x8 slice. The times are simulated.
256 devices in a mesh: band: 64 (over z, x, core), lev: 4 (over y).
Axes of the slice: x: 4, y: 4, z: 8, core: 2. Of those that a mesh axis runs over, the one named last changes fastest.
Arguments:
- columns: bfloat16 [524288, 274], P(('band', 'lev')), may hold values from -6 to 6
- departures: bfloat16 [4, 2048, 128, 616], P('lev', 'band'), may hold values from -6 to 6
- jacobian: bfloat16 [274, 616], replicated, may hold values from -0.375 to 0.375
- chan_precision: bfloat16 [616, 616], replicated, as said below
- send_rows: int32 [256, 256, 4], P(('band', 'lev')), may hold values from 0 to 2047
- obs_slot: int32 [4, 2048, 128], P('lev', 'band'), may hold values from 0 to 1023
- counts: int32 [4, 2048], P('lev', 'band'), may hold values from 16 to 128, as said below
Outputs:
- column_gradient: float32 [524288, 274], P(('band', 'lev'))
Inputs may be any that keep to these rules, and one draw needn't show every extreme that they name: `send_rows`: each entry names a column of the sending device. `obs_slot`: each entry names one of the 1024 slots, ordered by sending device then place. `counts`: each entry is 128 divided by 1, 2, 4 or 8; some entry equals 128. `chan_precision`: symmetric positive definite.
All inputs are finite; a program needn't handle non-finite values.
Results may differ from a plain program's by a relative error of at most 0.0018.
Values may be sent and summed in bfloat16 or wider, within the bound.
No kernel may reach another device: no remote copies, remote signals or barrier semaphores. Data moves between devices by JAX's collectives and lax.ppermute only.
A program may use at most 128 MiB of HBM per device.

v0:
```python
import math

import jax
import jax.numpy as jnp
from jax import lax
from jax.sharding import PartitionSpec as P

corr_length = 2.0


def extended(cells, sides, width):
    for axis, dim in sides:
        count = lax.axis_size(axis)
        ends = count - 1
        head = lax.slice_in_dim(cells, 0, width, axis=dim)
        tail = lax.slice_in_dim(cells, cells.shape[dim] - width, cells.shape[dim], axis=dim)
        cells = jnp.concatenate(
            [
                lax.ppermute(tail, axis, [(i, (i + 1) % count) for i in range(ends)]),
                cells,
                lax.ppermute(head, axis, [((i + 1) % count, i) for i in range(ends)]),
            ],
            axis=dim,
        )
    return cells


def on_device(columns, departures, jacobian, chan_precision, send_rows, obs_slot, counts):
    decay_rate = math.exp(-1.0 / corr_length)
    norm_factor = 1.0 / (1.0 - decay_rate * decay_rate)
    n_band = lax.axis_size("band")
    n_lev = lax.axis_size("lev")
    send_plan = send_rows[0]
    slot_depth = send_plan.shape[1]
    n_slots = send_plan.shape[0] * slot_depth
    prof_width = columns.shape[1]
    outgoing = columns[send_plan].reshape(n_band, n_lev, slot_depth, prof_width)
    arrived = lax.all_to_all(
        lax.all_to_all(outgoing, "band", split_axis=0, concat_axis=0, tiled=True),
        "lev",
        split_axis=1,
        concat_axis=1,
        tiled=True,
    )
    arrived_rows = arrived.reshape(n_slots, prof_width)
    line_deps = departures[0]
    n_lines, n_positions, n_chan = line_deps.shape
    slot_list = obs_slot[0].reshape(-1)
    obs_columns = arrived_rows[slot_list]
    model_equiv = jnp.dot(obs_columns, jacobian, preferred_element_type=jnp.float32)
    valid_mask = jnp.arange(n_positions, dtype=jnp.int32)[None, :] < counts[0][:, None]
    residual = jnp.where(
        valid_mask.reshape(-1, 1),
        model_equiv - line_deps.reshape(-1, n_chan).astype(jnp.float32),
        0.0,
    )
    residual = residual.astype(jnp.bfloat16)
    weighted = jnp.dot(residual, chan_precision, preferred_element_type=jnp.float32).reshape(
        n_lines, n_positions, n_chan
    )
    padded = extended(weighted, (("band", 0),), 1)
    previous = padded[:-2]
    following = padded[2:]
    global_line = lax.axis_index("band") * n_lines + jnp.arange(n_lines, dtype=jnp.int32)
    chain_length = n_band * n_lines
    at_end = (global_line == 0) | (global_line == chain_length - 1)
    chain_diag = jnp.where(at_end, norm_factor, (1.0 + decay_rate * decay_rate) * norm_factor)
    scaled = chain_diag[:, None, None] * weighted - decay_rate * norm_factor * (
        previous + following
    )
    scaled = jnp.where(valid_mask[:, :, None], scaled, 0.0).astype(jnp.bfloat16).reshape(-1, n_chan)
    obs_adjoint = lax.dot_general(
        scaled, jacobian, (((1,), (1,)), ((), ())), preferred_element_type=jnp.float32
    )
    adjoint_slots = jax.ops.segment_sum(obs_adjoint, slot_list, num_segments=n_slots)
    adjoint_slots = adjoint_slots.reshape(n_band, n_lev, slot_depth, prof_width)
    returned = lax.all_to_all(
        lax.all_to_all(adjoint_slots, "band", split_axis=0, concat_axis=0, tiled=True),
        "lev",
        split_axis=1,
        concat_axis=1,
        tiled=True,
    )
    return jax.ops.segment_sum(
        returned.reshape(n_slots, prof_width), send_plan.reshape(-1), num_segments=columns.shape[0]
    )


def solution(mesh):
    placed = (
        P(("band", "lev"), None),
        P("lev", "band", None, None),
        P(),
        P(),
        P(("band", "lev"), None, None),
        P("lev", "band", None),
        P("lev", "band"),
    )
    return jax.shard_map(
        on_device, mesh=mesh, in_specs=placed, out_specs=P(("band", "lev"), None), check_vma=False
    )
```

profile of v0, /device:TPU:1, one launch (start us, length us, event | category | flops | bytes accessed | tf_op | source)
XLA Modules:
  0.0 236.9 jit_solution(9502423091427595649)
XLA Ops:
  0.0 1.9 copy.21
  2.8 3.9 %gather_fusion = bf16[1024,274]{1,0:T(8,128)(2,1)S(1)} fusion(bf16[2048,274]{1,0:T(8,128)(2,1)S(1)} %copy.21, s32[1024]{0:T(1024)S(1)} %broadcast_clamp_fusion.1), kind=kCustom, calls=%fused_computation | custom fusion | bytes 1126400 | tf_op jit(solution)/shard_map/gather | solution.py:37
  7.9 13.0 %all-to-all-start = ((bf16[64,4,4,274]{3,2,1,0:T(4,128)(2,1)}), bf16[64,4,4,274]{3,2,1,0:T(4,128)(2,1)S(1)}, u32[]{:S(2)}, u32[]{:S(2)}) async-start(bf16[64,4,4,274]{3,2,1,0:T(4,128)(2,1)} %reshape.125), calls=%async_computation | async-start | bytes 1572864 | tf_op jit(solution)/shard_map/all_to_all | solution.py:39
  20.9 7.7 %copy.24 = f32[1,32,128,616]{2,1,3,0:T(8,128)} copy(bf16[1,32,128,616]{2,3,1,0:T(8,128)(2,1)} %param.8) | data formatting | bytes 15138816 | tf_op jit(solution)/shard_map/convert_element_type | solution.py:54
  28.6 15.3 %all-to-all-done = bf16[64,4,4,274]{3,2,1,0:T(4,128)(2,1)S(1)} async-done(((bf16[64,4,4,274]{3,2,1,0:T(4,128)(2,1)}), bf16[64,4,4,274]{3,2,1,0:T(4,128)(2,1)S(1)}, u32[]{:S(2)}, u32[]{:S(2)}) %all-to-all-start) | async-done | bytes 561184 | tf_op jit(solution)/shard_map/all_to_all | solution.py:39
  45.0 4.2 %all-to-all-start.1 = ((bf16[64,4,4,274]{3,2,0,1:T(4,128)(2,1)}), bf16[64,4,4,274]{3,2,0,1:T(4,128)(2,1)S(1)}, u32[]{:S(2)}, u32[]{:S(2)}) async-start(bf16[64,4,4,274]{3,2,0,1:T(4,128)(2,1)} %copy.22), calls=%async_computation.1 | async-start | bytes 1572864 | tf_op jit(solution)/shard_map/all_to_all | solution.py:38
  49.3 11.3 %all-to-all-done.1 = bf16[64,4,4,274]{3,2,0,1:T(4,128)(2,1)S(1)} async-done(((bf16[64,4,4,274]{3,2,0,1:T(4,128)(2,1)}), bf16[64,4,4,274]{3,2,0,1:T(4,128)(2,1)S(1)}, u32[]{:S(2)}, u32[]{:S(2)}) %all-to-all-start.1) | async-done | bytes 561184 | tf_op jit(solution)/shard_map/all_to_all | solution.py:38
  61.3 17.2 %gather_fusion.1 = bf16[4096,274]{1,0:T(8,128)(2,1)} fusion(bf16[1024,274]{1,0:T(8,128)(2,1)S(1)} %reshape.126, s32[4096]{0:T(1024)S(1)} %broadcast_clamp_fusion), kind=kCustom, calls=%fused_computation.1 | custom fusion | bytes 4505600 | tf_op jit(solution)/shard_map/gather | solution.py:49
  78.5 16.4 %fusion.12 = f32[4096,616]{0,1:T(8,128)} fusion(bf16[616,616]{1,0:T(8,128)(2,1)S(1)} %copy-done, f32[77,8,32,128]{3,2,1,0:T(8,128)} %bitcast.44, bf16[4096,274]{1,0:T(8,128)(2,1)} %gather_fusion.1, bf16[274,616]{1,0:T(8,128)(2,1)S(1)} %copy-done.5, pred[4096]{0:T(1024)(128)(4,1)S(1)} %get-tuple-element.8), kind=kOutput, calls=%fused_computation.19 | convolution fusion | flops 4498751488 | bytes 23530272 | tf_op jit(solution)/shard_map/dot_general | solution.py:58
  96.0 4.5 %collective-permute-start = (f32[1,128,616]{1,2,0:T(8,128)S(1)}, f32[1,128,616]{1,2,0:T(8,128)S(1)}, u32[]{:S(2)}, u32[]{:S(2)}) collective-permute-start(f32[1,128,616]{1,2,0:T(8,128)S(1)} %get-tuple-element.5), channel_id=1, source_target_pairs={{0,4},{4,8},{8,12},{12,16},{16,20},{20,24},{24,28},{28,32},{32,36}... | collective-permute-start | bytes 946184 | tf_op jit(solution)/shard_map/ppermute | solution.py:19
  100.5 2.1 collective-permute-start.1
  102.6 6.1 %copy.33 = f32[77,8,32,128]{3,2,1,0:T(8,128)S(1)} copy(f32[77,8,32,128]{3,1,2,0:T(8,128)} %bitcast.43) | data formatting | bytes 20185088
  108.8 5.1 %fusion.6 = bf16[32,128,616]{1,0,2:T(8,128)(2,1)S(1)} fusion(f32[1,128,616]{1,0,2:T(1,128)S(1)} %bitcast.47, f32[32,128,616]{1,0,2:T(8,128)S(1)} %bitcast.42, f32[1,128,616]{1,0,2:T(1,128)S(1)} %bitcast.46, f32[32]{0:T(128)S(1)} %or_select_fusion, pred[32,128]{1,0:T(8,128)(4,1)S(1)} %get-tuple-element.7), kind=kLoop, calls=%fused_computation.12 | loop fusion | flops 20185088 | bytes 15773824 | tf_op jit(solution)/shard_map/convert_element_type | solution.py:71
  113.9 8.3 %fusion.7 = f32[4096,274]{1,0:T(8,128)} fusion(bf16[274,616]{1,0:T(8,128)(2,1)S(1)} %copy-done.5, bf16[77,8,32,128]{3,2,1,0:T(8,128)(2,1)S(1)} %bitcast.45), kind=kOutput, calls=%fused_computation.14 | convolution fusion | flops 1382678528 | bytes 9873056 | tf_op jit(solution)/shard_map/dot_general | solution.py:72
  122.1 25.5 %scatter_custom_fusion = f32[1024,274]{1,0:T(8,128)S(1)} fusion(s32[4096]{0:T(1024)S(1)} %bitcast.50, f32[4096,274]{1,0:T(8,128)} %fusion.7, f32[]{:T(128)} %constant.11.clone.1), kind=kCustom, calls=%fused_computation.20 | custom fusion | flops 1122304 | bytes 1122816 | tf_op jit(solution)/shard_map/scatter-add | solution.py:75
  147.6 1.6 reshape.129
  149.2 48.4 %all_to_all.20 = f32[64,4,4,274]{3,2,1,0:T(4,128)S(1)} all-to-all(f32[64,4,4,274]{3,2,1,0:T(4,128)} %reshape.129), channel_id=1, replica_groups=mesh['band'=64,'lev'=4] {'band'}, dimensions={0} | all-to-all | bytes 2244608 | tf_op jit(solution)/shard_map/all_to_all | solution.py:78
  197.6 1.4 copy.28
  199.0 3.6 %all-to-all-start.3 = ((f32[64,4,4,274]{3,2,0,1:T(4,128)}), f32[64,4,4,274]{3,2,0,1:T(4,128)S(1)}, u32[]{:S(2)}, u32[]{:S(2)}) async-start(f32[64,4,4,274]{3,2,0,1:T(4,128)} %copy.28), calls=%async_computation.3 | async-start | bytes 3145728 | tf_op jit(solution)/shard_map/all_to_all | solution.py:77
  202.9 19.0 %all-to-all-done.3 = f32[64,4,4,274]{3,2,0,1:T(4,128)S(1)} async-done(((f32[64,4,4,274]{3,2,0,1:T(4,128)}), f32[64,4,4,274]{3,2,0,1:T(4,128)S(1)}, u32[]{:S(2)}, u32[]{:S(2)}) %all-to-all-start.3) | async-done | bytes 1122336 | tf_op jit(solution)/shard_map/all_to_all | solution.py:77
  221.9 1.4 copy.29
  223.3 1.9 reshape.160
  225.2 8.4 %scatter_custom_fusion.1 = f32[2048,274]{1,0:T(8,128)} fusion(s32[1024]{0:T(1024)S(1)} %reshape.158, f32[1024,274]{1,0:T(8,128)S(1)} %reshape.160, f32[]{:T(128)} %constant.11.clone.1), kind=kCustom, calls=%fused_computation.17 | custom fusion | flops 280576 | bytes 2244612 | tf_op jit(solution)/shard_map/scatter-add | solution.py:84
  233.6 3.3 %copy.30 = f32[2048,274]{0,1:T(8,128)} copy(f32[2048,274]{1,0:T(8,128)} %scatter_custom_fusion.1) | data formatting | bytes 4489216 | tf_op jit(solution)/shard_map/scatter-add | solution.py:84
  (29 shorter events, 5.4 us)
Async XLA Ops:
  0.0 78.5 %copy-start = (bf16[616,616]{1,0:T(8,128)(2,1)S(1)}, bf16[616,616]{1,0:T(8,128)(2,1)}, u32[]{:S(2)}) copy-start(bf16[616,616]{1,0:T(8,128)(2,1)} %param.10) | copy-start | bytes 2276740
  7.9 36.0 %all-to-all-start = ((bf16[64,4,4,274]{3,2,1,0:T(4,128)(2,1)}), bf16[64,4,4,274]{3,2,1,0:T(4,128)(2,1)S(1)}, u32[]{:S(2)}, u32[]{:S(2)}) async-start(bf16[64,4,4,274]{3,2,1,0:T(4,128)(2,1)} %reshape.125), calls=%async_computation | async-start | bytes 1572864 | tf_op jit(solution)/shard_map/all_to_all | solution.py:39
  20.8 7.7 %copy-start.3 = (s32[1,32,128]{2,1,0:T(8,128)S(1)}, s32[1,32,128]{2,1,0:T(8,128)}, u32[]{:S(2)}) copy-start(s32[1,32,128]{2,1,0:T(8,128)} %param.12) | copy-start | bytes 49156
  20.9 28.3 %copy-start.4 = (s32[1,32]{1,0:T(1,128)S(1)}, s32[1,32]{1,0:T(1,128)}, u32[]{:S(2)}) copy-start(s32[1,32]{1,0:T(1,128)} %param.13) | copy-start | bytes 388
  45.0 15.6 %all-to-all-start.1 = ((bf16[64,4,4,274]{3,2,0,1:T(4,128)(2,1)}), bf16[64,4,4,274]{3,2,0,1:T(4,128)(2,1)S(1)}, u32[]{:S(2)}, u32[]{:S(2)}) async-start(bf16[64,4,4,274]{3,2,0,1:T(4,128)(2,1)} %copy.22), calls=%async_computation.1 | async-start | bytes 1572864 | tf_op jit(solution)/shard_map/all_to_all | solution.py:38
  61.3 17.2 %copy-start.5 = (bf16[274,616]{1,0:T(8,128)(2,1)S(1)}, bf16[274,616]{1,0:T(8,128)(2,1)}, u32[]{:S(2)}) copy-start(bf16[274,616]{1,0:T(8,128)(2,1)} %param.9) | copy-start | bytes 1012708
  96.0 12.7 %collective-permute-start = (f32[1,128,616]{1,2,0:T(8,128)S(1)}, f32[1,128,616]{1,2,0:T(8,128)S(1)}, u32[]{:S(2)}, u32[]{:S(2)}) collective-permute-start(f32[1,128,616]{1,2,0:T(8,128)S(1)} %get-tuple-element.5), channel_id=1, source_target_pairs={{0,4},{4,8},{8,12},{12,16},{16,20},{20,24},{24,28},{28,32},{32,36}... | collective-permute-start | bytes 946184 | tf_op jit(solution)/shard_map/ppermute | solution.py:19
  100.5 8.3 %collective-permute-start.1 = (f32[1,128,616]{1,2,0:T(8,128)S(1)}, f32[1,128,616]{1,2,0:T(8,128)S(1)}, u32[]{:S(2)}, u32[]{:S(2)}) collective-permute-start(f32[1,128,616]{1,2,0:T(8,128)S(1)} %get-tuple-element.6), channel_id=1, source_target_pairs={{4,0},{8,4},{12,8},{16,12},{20,16},{24,20},{28,24},{32,28},{36,32}... | collective-permute-start | bytes 946184 | tf_op jit(solution)/shard_map/ppermute | solution.py:21
  149.2 53.3 %copy-start.2 = (s32[1,256,4]{1,2,0:T(4,128)S(1)}, s32[1,256,4]{1,2,0:T(4,128)}, u32[]{:S(2)}) copy-start(s32[1,256,4]{1,2,0:T(4,128)} %param.11) | copy-start | bytes 12292
  199.0 22.8 %all-to-all-start.3 = ((f32[64,4,4,274]{3,2,0,1:T(4,128)}), f32[64,4,4,274]{3,2,0,1:T(4,128)S(1)}, u32[]{:S(2)}, u32[]{:S(2)}) async-start(f32[64,4,4,274]{3,2,0,1:T(4,128)} %copy.28), calls=%async_computation.3 | async-start | bytes 3145728 | tf_op jit(solution)/shard_map/all_to_all | solution.py:77
  223.3 13.6 %copy-start.1 = (bf16[616,616]{1,0:T(8,128)(2,1)S(1)}, bf16[616,616]{1,0:T(8,128)(2,1)}, u32[]{:S(2)}) copy-start(bf16[616,616]{1,0:T(8,128)(2,1)} %param.10) | copy-start | bytes 2276740
where the time goes:
time: 238 us; the launch traced here: 237 us
  local copies, waits for them, and re-layouts  51 us (21%)
  blocking collectives  48.4 us (20%)
  waiting for transfers between devices  45.6 us (19%)
  other arithmetic  39.8 us (17%)
  starting transfers between devices  27.3 us (11%)
  matrix products  24.7 us (10%)
    all_to_all x1, blocking collectives, on_device(): lax.all_to_all(adjoint_slots, 'band', split_axis=0, concat_axis=0, tiled=...  48.4 us
    scatter-add x1, other arithmetic, on_device(): jax.ops.segment_sum(obs_adjoint, slot_list, num_segments=n_slots)  25.5 us
    all_to_all x1, waiting for transfers between devices, on_device(): lax.all_to_all(lax.all_to_all(adjoint_slots, 'band', split_axis=0, concat...  19 us
    gather x1, local copies, waits for them, and re-layouts, on_device(): obs_columns = arrived_rows[slot_list]  17.2 us
    dot_general x1, matrix products, on_device(): jnp.dot(residual, chan_precision, preferred_element_type=jnp.float32)  16.4 us
    all_to_all x1, waiting for transfers between devices, on_device(): lax.all_to_all(outgoing, 'band', split_axis=0, concat_axis=0, tiled=True)  15.3 us
    all_to_all x1, starting transfers between devices, on_device(): lax.all_to_all(outgoing, 'band', split_axis=0, concat_axis=0, tiled=True)  13 us
    all_to_all x1, waiting for transfers between devices, on_device(): lax.all_to_all(lax.all_to_all(outgoing, 'band', split_axis=0, concat_axis...  11.3 us
  transfers between devices with their start and end apart: 5, of which 3 were waited for; matrix products, arithmetic and copies ran while one was open for 6% of the time, Pallas kernels for 0%

commit v1 on v0

v1 whole, which is shorter than its diff:
```python
import functools
import math

import jax
import jax.numpy as jnp
from jax import lax
from jax.experimental import pallas as pl
from jax.experimental.pallas import tpu as pltpu
from jax.sharding import PartitionSpec as P

corr_length = 2.0
BF, F32 = jnp.bfloat16, jnp.float32
NT = (((1,), (1,)), ((), ()))
VMEM = pl.BlockSpec(memory_space=pltpu.VMEM)
SMEM = pl.BlockSpec(memory_space=pltpu.SMEM)
LIMIT = 58 * 1024 * 1024
MAIN, TAIL_AT, TAIL_STEP, WIRE = 256, 512, 64, 640


def mm(a, b):
    return jnp.dot(a, b, preferred_element_type=F32)


def mm_nt(a, b):
    return lax.dot_general(a, b, NT, preferred_element_type=F32)


def one_hot_t(rows, idx):
    n = idx.shape[1]
    row = lax.broadcasted_iota(jnp.int32, (rows, n), 0)
    return jnp.where(row == idx, 1.0, 0.0).astype(BF)


def store_wire(wire, c, block, prof):
    r, par = c // 2, c % 2
    n = block.shape[1]
    wire[r, :, par * MAIN : (par + 1) * MAIN] = block[:MAIN].T.astype(BF)
    tail = jnp.concatenate([block[MAIN:], jnp.zeros((TAIL_STEP - (prof - MAIN), n), block.dtype)], axis=0)
    return tail


def pack_wire(wire, blocks, prof):
    for r in range(2):
        tails = [store_wire(wire, 2 * r + par, blocks[2 * r + par], prof) for par in range(2)]
        wire[r, :, TAIL_AT:] = jnp.concatenate(tails, axis=0).T.astype(BF)


def unpack_wire(wire, out, prof):
    n = wire.shape[1]
    for r in range(2):
        turned = wire[r].astype(F32).T.astype(BF)
        for par in range(2):
            c = 2 * r + par
            out[0:MAIN, c * n : (c + 1) * n] = turned[par * MAIN : (par + 1) * MAIN]
            at = TAIL_AT + par * TAIL_STEP
            out[MAIN:prof, c * n : (c + 1) * n] = turned[at : at + prof - MAIN]


def send_kernel(cols, plan, wire):
    prof, n_cols = cols.shape
    blocks = [mm(cols[...], one_hot_t(n_cols, plan[c : c + 1, :])) for c in range(4)]
    pack_wire(wire, blocks, prof)


def edge_kernel(wire, slot, valid, dep, jac_t, arrived, resid):
    prof = arrived.shape[0]
    unpack_wire(wire, arrived, prof)
    n_slots = arrived.shape[1]
    n_pos = dep.shape[2]
    last = dep.shape[0] - 1
    for side, line in ((0, 0), (1, last)):
        at = line * n_pos
        hot = one_hot_t(n_slots, slot[:, at : at + n_pos])
        obs = mm(arrived[...], hot).astype(BF)
        model = mm(jac_t[...], obs)
        res = jnp.where(valid[:, at : at + n_pos] > 0, model - dep[line].astype(F32), 0.0)
        resid[:, side * n_pos : (side + 1) * n_pos] = res.astype(BF)


def main_kernel(rf, inner, arrived, slot, valid, dep, jac_t, prec, part, edges, hot_s, w_s, sc_s):
    n_slots = arrived.shape[1]
    n_lines, n_chan, n_pos = dep.shape
    group = 4
    width = group * n_pos

    @pl.loop(0, n_lines // group)
    def _(j):
        at = pl.multiple_of(j * width, width)
        hot = one_hot_t(n_slots, slot[:, pl.ds(at, width)])
        hot_s[:, pl.ds(at, width)] = hot
        obs = mm(arrived[...], hot).astype(BF)
        model = mm(jac_t[...], obs)
        deps = jnp.concatenate([dep[j * group + g] for g in range(group)], axis=1)
        res = jnp.where(valid[:, pl.ds(at, width)] > 0, model - deps.astype(F32), 0.0)
        w_s[:, pl.ds(at, width)] = mm(prec[...], res.astype(BF))

    total = n_lines * n_pos
    zero = jnp.zeros((n_chan, n_pos), BF)
    sc_s[:, 0:n_pos] = zero
    sc_s[:, total - n_pos : total] = zero

    @pl.loop(1, n_lines - 1)
    def _(i):
        at = pl.multiple_of(i * n_pos, n_pos)
        before = w_s[:, pl.ds(at - n_pos, n_pos)]
        after = w_s[:, pl.ds(at + n_pos, n_pos)]
        val = inner * w_s[:, pl.ds(at, n_pos)] - rf * (before + after)
        sc_s[:, pl.ds(at, n_pos)] = jnp.where(valid[:, pl.ds(at, n_pos)] > 0, val, 0.0).astype(BF)

    edges[:, 0 : 2 * n_pos] = w_s[:, 0 : 2 * n_pos]
    edges[:, 2 * n_pos :] = w_s[:, total - 2 * n_pos :]

    step = min(256, n_slots)
    @pl.loop(0, n_slots // step)
    def _(q):
        at = pl.multiple_of(q * step, step)
        part[:, pl.ds(at, step)] = mm_nt(sc_s[...], hot_s[pl.ds(at, step), :])


def finish_kernel(rf, diag, halo, edges, slot, valid, part, jac, prec, wire):
    prof = jac.shape[0]
    n_slots = part.shape[1]
    n_pos = halo.shape[1] // 2
    total = slot.shape[1]
    outer = mm(prec[...], halo[...])
    ends = []
    for side, line_at in ((0, 0), (1, total - n_pos)):
        own = edges[:, 3 * side * n_pos : (3 * side + 1) * n_pos]
        inside = edges[:, (1 + side) * n_pos : (2 + side) * n_pos]
        beyond = outer[:, side * n_pos : (side + 1) * n_pos]
        val = diag[side] * own - rf * (inside + beyond)
        ends.append(jnp.where(valid[:, line_at : line_at + n_pos] > 0, val, 0.0).astype(BF))
    scaled = jnp.concatenate(ends, axis=1)
    idx = jnp.concatenate([slot[:, 0:n_pos], slot[:, total - n_pos :]], axis=1)
    blocks = []
    step = n_slots // 4
    for c in range(4):
        row = lax.broadcasted_iota(jnp.int32, (step, 2 * n_pos), 0) + c * step
        hot = jnp.where(row == idx, 1.0, 0.0).astype(BF)
        sums = part[:, c * step : (c + 1) * step] + mm_nt(scaled, hot)
        high = sums.astype(BF)
        low = (sums - high.astype(F32)).astype(BF)
        blocks.append(mm(jac[...], high) + mm(jac[...], low))
    pack_wire(wire, blocks, prof)


def collect_kernel(wire, plan, grad, back):
    prof = back.shape[0]
    unpack_wire(wire, back, prof)
    n = plan.shape[1]
    step = min(512, grad.shape[1])

    @pl.loop(0, grad.shape[1] // step)
    def _(q):
        at = pl.multiple_of(q * step, step)
        hots = []
        for c in range(4):
            row = lax.broadcasted_iota(jnp.int32, (step, n), 0) + at
            hots.append(jnp.where(row == plan[c : c + 1, :], 1.0, 0.0).astype(BF))
        grad[:, pl.ds(at, step)] = mm_nt(back[...], jnp.concatenate(hots, axis=1))


def call(body, outs, n_in, scratch=(), smem=()):
    specs = [SMEM if i in smem else VMEM for i in range(n_in)]
    return pl.pallas_call(
        body,
        out_shape=outs,
        in_specs=specs,
        out_specs=[VMEM] * len(outs),
        scratch_shapes=list(scratch),
        compiler_params=pltpu.CompilerParams(vmem_limit_bytes=LIMIT),
    )


def on_device(columns, departures, jacobian, chan_precision, send_rows, obs_slot, counts):
    decay = math.exp(-1.0 / corr_length)
    norm = 1.0 / (1.0 - decay * decay)
    rf, inner = decay * norm, (1.0 + decay * decay) * norm
    n_band = lax.axis_size("band")
    n_dev = n_band * lax.axis_size("lev")
    n_cols, prof = columns.shape
    _, n_lines, n_pos, n_chan = departures.shape
    total = n_lines * n_pos
    depth = send_rows.shape[2]
    n_slots = n_dev * depth
    sds = jax.ShapeDtypeStruct

    plan = send_rows[0].T
    jac_t = jacobian.T
    dep = departures[0].transpose(0, 2, 1)
    slots = obs_slot[0].reshape(1, total)
    slots = (slots % depth) * n_dev + slots // depth
    valid = jnp.arange(n_pos, dtype=jnp.int32)[None, :] < counts[0][:, None]
    valid = valid.astype(jnp.int32).reshape(1, total)

    wire_shape = sds((2, n_dev, WIRE), BF)

    def exchange(wire):
        sent = wire.transpose(1, 0, 2)
        got = lax.all_to_all(sent, ("band", "lev"), split_axis=0, concat_axis=0, tiled=True)
        return got.transpose(1, 0, 2)

    (wire,) = call(send_kernel, [wire_shape], 2)(columns.T, plan)
    got = exchange(wire)
    arrived, resid = call(
        edge_kernel, [sds((prof, n_slots), BF), sds((n_chan, 2 * n_pos), BF)], 5
    )(got, slots, valid, dep, jac_t)
    ends = n_band - 1
    from_before = lax.ppermute(resid[:, n_pos:], "band", [(i, i + 1) for i in range(ends)])
    from_after = lax.ppermute(resid[:, :n_pos], "band", [(i + 1, i) for i in range(ends)])
    part, edges = call(
        functools.partial(main_kernel, rf, inner),
        [sds((n_chan, n_slots), F32), sds((n_chan, 4 * n_pos), F32)],
        6,
        scratch=[
            pltpu.VMEM((n_slots, total), BF),
            pltpu.VMEM((n_chan, total), F32),
            pltpu.VMEM((n_chan, total), BF),
        ],
    )(arrived, slots, valid, dep, jac_t, chan_precision)
    halo = jnp.concatenate([from_before, from_after], axis=1)
    band = lax.axis_index("band")
    diag = jnp.stack([jnp.where(band == 0, norm, inner), jnp.where(band == ends, norm, inner)]).astype(F32)
    (wire,) = call(functools.partial(finish_kernel, rf), [wire_shape], 8, smem=(0,))(
        diag, halo, edges, slots, valid, part, jacobian, chan_precision
    )
    back = exchange(wire)
    (grad,) = call(
        collect_kernel, [sds((prof, n_cols), F32)], 2, scratch=[pltpu.VMEM((prof, n_slots), BF)]
    )(back, plan)
    return grad.T


def solution(mesh):
    placed = (
        P(("band", "lev"), None),
        P("lev", "band", None, None),
        P(),
        P(),
        P(("band", "lev"), None, None),
        P("lev", "band", None),
        P("lev", "band"),
    )
    return jax.shard_map(
        on_device, mesh=mesh, in_specs=placed, out_specs=P(("band", "lev"), None), check_vma=False
    )
```

time: 238 us -> 130 us (0.55)
  Pallas kernels: 0 us -> 46.3 us
  local copies, waits for them, and re-layouts: 51 us -> 8.18 us
  other arithmetic: 39.8 us -> 2.69 us
  waiting for transfers between devices: 45.6 us -> 20.3 us
  matrix products: 24.7 us -> 0 us
  blocking collectives: 48.4 us -> 32.4 us
  starting transfers between devices: 27.3 us -> 20 us
    pallas_call x0 -> x5, Pallas kernels: none -> 46.3 us  [the longest x1 27.3 us: on_device(): call(functools.partial(main_kernel, rf, inner), [sds((n_chan, n_slots), F...]
    scatter-add x2 -> x0, other arithmetic: 33.9 us -> none  [the longest x1 25.5 us: on_device(): jax.ops.segment_sum(obs_adjoint, slot_list, num_segments=n_slots)]
    all_to_all x3 -> x1, waiting for transfers between devices: 45.6 us -> 20.3 us  [exchange(): lax.all_to_all(sent, ('band', 'lev'), split_axis=0, concat_axis=0, tiled=...]
    dot_general x2 -> x0, matrix products: 24.7 us -> none  [the longest x1 16.4 us: on_device(): jnp.dot(residual, chan_precision, preferred_element_type=jnp.float32)]
    gather x2 -> x0, local copies, waits for them, and re-layouts: 21.1 us -> none  [the longest x1 17.2 us: on_device(): obs_columns = arrived_rows[slot_list]]
    all_to_all x1, blocking collectives: 48.4 us -> 32.4 us  [exchange(): lax.all_to_all(sent, ('band', 'lev'), split_axis=0, concat_axis=0, tiled=...]
    convert_element_type x1 -> x0, local copies, waits for them, and re-layouts: 7.68 us -> none  [on_device(): line_deps.reshape(-1, n_chan).astype(jnp.float32)]
    unnamed x15 -> x7, local copies, waits for them, and re-layouts: 8.17 us -> 0.99 us
  transfers between devices with their start and end apart: 5 -> 3, of which waited for: 3 -> 1; matrix products, arithmetic and copies ran while one was open for 6% -> 2% of each run, Pallas kernels for 0% -> 21%
where the time goes in v1:
time: 130 us
  Pallas kernels  46.3 us (36%)
  blocking collectives  32.4 us (25%)
  waiting for transfers between devices  20.3 us (16%)
  starting transfers between devices  20 us (15%)
  local copies, waits for them, and re-layouts  8.18 us (6%)
  other arithmetic  2.69 us (2%)
    all_to_all x1, blocking collectives, exchange(): lax.all_to_all(sent, ('band', 'lev'), split_axis=0, concat_axis=0, tiled=...  32.4 us
    pallas_call x1, Pallas kernels, on_device(): call(functools.partial(main_kernel, rf, inner), [sds((n_chan, n_slots), F...  27.3 us
    all_to_all x1, waiting for transfers between devices, exchange(): lax.all_to_all(sent, ('band', 'lev'), split_axis=0, concat_axis=0, tiled=...  20.3 us
    all_to_all x1, starting transfers between devices, exchange(): lax.all_to_all(sent, ('band', 'lev'), split_axis=0, concat_axis=0, tiled=...  15.6 us
    pallas_call x1, Pallas kernels, on_device(): call(functools.partial(finish_kernel, rf), [wire_shape], 8, smem=(0,))  5.81 us
    pallas_call x1, Pallas kernels, on_device(): call(collect_kernel, [sds((prof, n_cols), F32)], 2, scratch=[pltpu.VMEM((...  4.73 us
    pallas_call x1, Pallas kernels, on_device(): call(edge_kernel, [sds((prof, n_slots), BF), sds((n_chan, 2 * n_pos), BF)...  4.71 us
    transpose x2, local copies, waits for them, and re-layouts, exchange(): sent = wire.transpose(1, 0, 2)  4.36 us
  transfers between devices with their start and end apart: 3, of which 1 were waited for; matrix products, arithmetic and copies ran while one was open for 2% of the time, Pallas kernels for 21%

profile of v1, /device:TPU:1, one launch (start us, length us, event | category | flops | bytes accessed | tf_op | source)
XLA Modules:
  0.0 129.8 jit_solution(11167628533752096272)
XLA Ops:
  0.0 3.7 %shard_map.73 = bf16[2,256,640]{2,1,0:T(8,128)(2,1)} custom-call(bf16[274,2048]{1,0:T(8,128)(2,1)} %bitcast.30, s32[4,256]{1,0:T(4,128)} %bitcast.34), custom_call_target="tpu_custom_call" | custom-call | tf_op jit(solution)/shard_map/pallas_call | solution.py:203
  3.7 2.6 %copy.9 = bf16[256,2,640]{2,1,0:T(2,128)(2,1)} copy(bf16[256,2,640]{2,0,1:T(8,128)(2,1)} %bitcast.27) | data formatting | bytes 1310720 | tf_op jit(solution)/shard_map/transpose | solution.py:199
  6.3 15.6 %all-to-all-start = ((bf16[256,2,640]{2,1,0:T(2,128)(2,1)}), bf16[256,2,640]{2,1,0:T(2,128)(2,1)S(1)}, u32[]{:S(2)}, u32[]{:S(2)}) async-start(bf16[256,2,640]{2,1,0:T(2,128)(2,1)} %copy.9), calls=%async_computation | async-start | bytes 1310720 | tf_op jit(solution)/shard_map/all_to_all | solution.py:200
  21.9 0.0 copy-done
  21.9 1.0 copy.11
  22.9 0.0 copy-done.2
  22.9 0.7 fusion.2
  23.6 0.7 fusion.1.slot
  24.3 20.3 %all-to-all-done = bf16[256,2,640]{2,1,0:T(2,128)(2,1)S(1)} async-done(((bf16[256,2,640]{2,1,0:T(2,128)(2,1)}), bf16[256,2,640]{2,1,0:T(2,128)(2,1)S(1)}, u32[]{:S(2)}, u32[]{:S(2)}) %all-to-all-start) | async-done | bytes 655392 | tf_op jit(solution)/shard_map/all_to_all | solution.py:200
  44.6 0.9 copy.17
  45.5 4.7 %shard_map.74 = (bf16[274,1024]{1,0:T(8,128)(2,1)}, bf16[616,256]{1,0:T(8,128)(2,1)}) custom-call(bf16[2,256,640]{2,1,0:T(8,128)(2,1)} %bitcast.26, s32[1,4096]{1,0:T(1,128)} %fusion.1.slot, s32[1,4096]{1,0:T(1,128)} %bitcast.31, bf16[32,616,128]{2,1,0:T(8,128)(2,1)} %bitcast.22, bf16[616,274]{1,0:T(8,128)(2,1)} %bitcast.24), custom_call_target="tpu_custom_call" | custom-call | tf_op jit(solution)/shard_map/pallas_call | solution.py:205
  50.2 1.0 fusion.3
  51.2 2.4 %collective-permute-start = (bf16[616,128]{1,0:T(8,128)(2,1)S(1)}, bf16[616,128]{1,0:T(8,128)(2,1)S(1)}, u32[]{:S(2)}, u32[]{:S(2)}) collective-permute-start(bf16[616,128]{1,0:T(8,128)(2,1)S(1)} %get-tuple-element.13), channel_id=1, source_target_pairs={{0,4},{4,8},{8,12},{12,16},{16,20},{20,24},{24,28},{28,32},{32,36}... | collective-permute-start | bytes 473096 | tf_op jit(solution)/shard_map/ppermute | solution.py:209
  53.6 1.9 %collective-permute-start.1 = (bf16[616,128]{1,0:T(8,128)(2,1)S(1)}, bf16[616,128]{1,0:T(8,128)(2,1)S(1)}, u32[]{:S(2)}, u32[]{:S(2)}) collective-permute-start(bf16[616,128]{1,0:T(8,128)(2,1)S(1)} %get-tuple-element.14), channel_id=1, source_target_pairs={{4,0},{8,4},{12,8},{16,12},{20,16},{24,20},{28,24},{32,28},{36,32}... | collective-permute-start | bytes 473096 | tf_op jit(solution)/shard_map/ppermute | solution.py:210
  55.6 0.6 pad_maximum_fusion.1.diag
  56.1 27.3 %shard_map.75 = (f32[616,1024]{1,0:T(8,128)}, f32[616,512]{1,0:T(8,128)}) custom-call(bf16[274,1024]{1,0:T(8,128)(2,1)} %get-tuple-element.10.arrived, s32[1,4096]{1,0:T(1,128)} %fusion.1.slot, s32[1,4096]{1,0:T(1,128)} %bitcast.32, bf16[32,616,128]{2,1,0:T(8,128)(2,1)} %bitcast.23, bf16[616,274]{1,0:T(8,128)(2,1)} %bitcast.25, bf16[616,616]{1,0:T(8,128)(2,1)} %prec.3), custom_call_target="tpu_custom_call" | custom-call | tf_op jit(solution)/shard_map/pallas_call | solution.py:211
  83.5 0.0 collective-permute-done
  83.5 0.0 collective-permute-done.1
  83.5 0.7 pad_maximum_fusion.halo
  84.2 5.8 %shard_map.76 = bf16[2,256,640]{2,1,0:T(8,128)(2,1)} custom-call(f32[2]{0:T(128)} %pad_maximum_fusion.1.diag, bf16[616,256]{1,0:T(8,128)(2,1)} %pad_maximum_fusion.halo, f32[616,512]{1,0:T(8,128)} %get-tuple-element.11.edges, s32[1,4096]{1,0:T(1,128)} %fusion.1.slot, s32[1,4096]{1,0:T(1,128)} %bitcast.33, f32[616,1024]{1,0:T(8,128)} %get-tuple-element.12.part, ...), custom_call_target="tpu_custom_call" | custom-call | tf_op jit(solution)/shard_map/pallas_call | solution.py:224
  90.0 1.8 %copy.12 = bf16[256,2,640]{2,1,0:T(2,128)(2,1)S(1)} copy(bf16[256,2,640]{2,0,1:T(8,128)(2,1)} %bitcast.29) | data formatting | bytes 1310720 | tf_op jit(solution)/shard_map/transpose | solution.py:199
  91.8 32.4 %all_to_all.10 = bf16[256,2,640]{2,1,0:T(2,128)(2,1)S(1)} all-to-all(bf16[256,2,640]{2,1,0:T(2,128)(2,1)S(1)} %copy.12), channel_id=1, replica_groups=mesh['band'=64,'lev'=4] {'band','lev'}, dimensions={0} | all-to-all | bytes 1310720 | tf_op jit(solution)/shard_map/all_to_all | solution.py:200
  124.2 0.9 copy.16
  125.1 4.7 %shard_map.77 = f32[274,2048]{1,0:T(8,128)} custom-call(bf16[2,256,640]{2,1,0:T(8,128)(2,1)} %bitcast.28, s32[4,256]{1,0:T(4,128)} %bitcast.35), custom_call_target="tpu_custom_call" | custom-call | tf_op jit(solution)/shard_map/pallas_call | solution.py:228
  (4 shorter events, 0.0 us)
Async XLA Ops:
  0.0 21.9 %copy-start = (bf16[274,616]{1,0:T(8,128)(2,1)S(1)}, bf16[274,616]{1,0:T(8,128)(2,1)}, u32[]{:S(2)}) copy-start(bf16[274,616]{1,0:T(8,128)(2,1)} %jac.1) | copy-start | bytes 1012708
  0.0 22.9 %copy-start.2 = (s32[1,32]{1,0:T(1,128)S(1)}, s32[1,32]{1,0:T(1,128)}, u32[]{:S(2)}) copy-start(s32[1,32]{1,0:T(1,128)} %param.13) | copy-start | bytes 388
  0.0 23.6 %copy-start.1 = (s32[1,32,128]{2,1,0:T(8,128)S(1)}, s32[1,32,128]{2,1,0:T(8,128)}, u32[]{:S(2)}) copy-start(s32[1,32,128]{2,1,0:T(8,128)} %param.12) | copy-start | bytes 49156
  6.3 38.3 %all-to-all-start = ((bf16[256,2,640]{2,1,0:T(2,128)(2,1)}), bf16[256,2,640]{2,1,0:T(2,128)(2,1)S(1)}, u32[]{:S(2)}, u32[]{:S(2)}) async-start(bf16[256,2,640]{2,1,0:T(2,128)(2,1)} %copy.9), calls=%async_computation | async-start | bytes 1310720 | tf_op jit(solution)/shard_map/all_to_all | solution.py:200
  51.2 32.2 %collective-permute-start = (bf16[616,128]{1,0:T(8,128)(2,1)S(1)}, bf16[616,128]{1,0:T(8,128)(2,1)S(1)}, u32[]{:S(2)}, u32[]{:S(2)}) collective-permute-start(bf16[616,128]{1,0:T(8,128)(2,1)S(1)} %get-tuple-element.13), channel_id=1, source_target_pairs={{0,4},{4,8},{8,12},{12,16},{16,20},{20,24},{24,28},{28,32},{32,36}... | collective-permute-start | bytes 473096 | tf_op jit(solution)/shard_map/ppermute | solution.py:209
  53.6 29.8 %collective-permute-start.1 = (bf16[616,128]{1,0:T(8,128)(2,1)S(1)}, bf16[616,128]{1,0:T(8,128)(2,1)S(1)}, u32[]{:S(2)}, u32[]{:S(2)}) collective-permute-start(bf16[616,128]{1,0:T(8,128)(2,1)S(1)} %get-tuple-element.14), channel_id=1, source_target_pairs={{4,0},{8,4},{12,8},{16,12},{20,16},{24,20},{28,24},{32,28},{36,32}... | collective-permute-start | bytes 473096 | tf_op jit(solution)/shard_map/ppermute | solution.py:210

commit v2 on v1

v2 whole, which is shorter than its diff:
```python
import functools
import math

import jax
import jax.numpy as jnp
from jax import lax
from jax.experimental import pallas as pl
from jax.experimental.pallas import tpu as pltpu
from jax.sharding import PartitionSpec as P

corr_length = 2.0
BF, F32 = jnp.bfloat16, jnp.float32
NT = (((1,), (1,)), ((), ()))
VMEM = pl.BlockSpec(memory_space=pltpu.VMEM)
SMEM = pl.BlockSpec(memory_space=pltpu.SMEM)
HBM = pl.BlockSpec(memory_space=pltpu.HBM)
MIB = 1024 * 1024
MAIN, TAIL_AT, TAIL_STEP, WIRE = 256, 512, 64, 640


def mm(a, b):
    return jnp.dot(a, b, preferred_element_type=F32)


def mm_nt(a, b):
    return lax.dot_general(a, b, NT, preferred_element_type=F32)


def one_hot_t(rows, idx):
    n = idx.shape[1]
    row = lax.broadcasted_iota(jnp.int32, (rows, n), 0)
    return jnp.where(row == idx, 1.0, 0.0).astype(BF)


def store_wire(wire, c, block, prof):
    r, par = c // 2, c % 2
    n = block.shape[1]
    wire[r, :, par * MAIN : (par + 1) * MAIN] = block[:MAIN].T.astype(BF)
    tail = jnp.concatenate([block[MAIN:], jnp.zeros((TAIL_STEP - (prof - MAIN), n), block.dtype)], axis=0)
    return tail


def pack_wire(wire, blocks, prof):
    for r in range(2):
        tails = [store_wire(wire, 2 * r + par, blocks[2 * r + par], prof) for par in range(2)]
        wire[r, :, TAIL_AT:] = jnp.concatenate(tails, axis=0).T.astype(BF)


def unpack_wire(wire, out, prof):
    n = wire.shape[1]
    for r in range(2):
        turned = wire[r].astype(F32).T.astype(BF)
        for par in range(2):
            c = 2 * r + par
            out[0:MAIN, c * n : (c + 1) * n] = turned[par * MAIN : (par + 1) * MAIN]
            at = TAIL_AT + par * TAIL_STEP
            out[MAIN:prof, c * n : (c + 1) * n] = turned[at : at + prof - MAIN]


def send_kernel(cols_in, plan, wire, hot, cols, sem):
    prof, n_cols = cols.shape
    copy = pltpu.make_async_copy(cols_in, cols, sem)
    copy.start()
    n = plan.shape[1]
    for c in range(4):
        hot[:, c * n : (c + 1) * n] = one_hot_t(n_cols, plan[c : c + 1, :])
    copy.wait()
    blocks = [mm(cols[...], hot[:, c * n : (c + 1) * n]) for c in range(4)]
    pack_wire(wire, blocks, prof)


def hot_kernel(slot, hot):
    width = 512

    @pl.loop(0, hot.shape[1] // width)
    def _(j):
        at = pl.multiple_of(j * width, width)
        hot[:, pl.ds(at, width)] = one_hot_t(hot.shape[0], slot[:, pl.ds(at, width)])


def hot_plan_kernel(plan, hot):
    n = plan.shape[1]
    for c in range(4):
        hot[:, c * n : (c + 1) * n] = one_hot_t(hot.shape[0], plan[c : c + 1, :])


def edge_kernel(wire, slot, valid, dep, jac_t, arrived, first, last, deps, sems):
    copies = [
        pltpu.make_async_copy(dep.at[line], deps.at[k], sems.at[k]) for k, line in enumerate((0, dep.shape[0] - 1))
    ]
    for copy in copies:
        copy.start()
    prof, n_slots = arrived.shape
    unpack_wire(wire, arrived, prof)
    n_pos = dep.shape[2]
    end = slot.shape[1] - n_pos
    idx = jnp.concatenate([slot[:, :n_pos], slot[:, end:]], axis=1)
    obs = mm(arrived[...], one_hot_t(n_slots, idx)).astype(BF)
    model = mm(jac_t[...], obs)
    for k, at, out in ((0, 0, first), (1, end, last)):
        copies[k].wait()
        res = model[:, k * n_pos : (k + 1) * n_pos] - deps[k].astype(F32)
        out[...] = jnp.where(valid[:, at : at + n_pos] > 0, res, 0.0).astype(BF)


def main_kernel(rf, inner, arrived, hot_in, valid, dep, jac_t, prec, first, last, part, edges, *scratch):
    w_s, sc_s, deps, hot, sems = scratch[:5]
    obs_s, res_s = scratch[5:7], scratch[7:]
    n_slots = arrived.shape[1]
    n_lines, n_chan, n_pos = dep.shape
    total = n_lines * n_pos
    groups = []
    line = 1
    while line < n_lines - 1:
        size = min(4, n_lines - 1 - line)
        groups.append((line, size))
        line += size
    copies = []
    for g, (line, size) in enumerate(groups):
        span, lanes = pl.ds(line, size), pl.ds(line * n_pos, size * n_pos)
        pair = (
            pltpu.make_async_copy(hot_in.at[:, lanes], hot.at[:, lanes], sems.at[0, g]),
            pltpu.make_async_copy(dep.at[span], deps.at[span], sems.at[1, g]),
        )
        for copy in pair:
            copy.start()
        copies.append(pair)

    def gather(g):
        line, size = groups[g]
        lanes = slice(line * n_pos, (line + size) * n_pos)
        copies[g][0].wait()
        obs_s[g % 2][:, : size * n_pos] = mm(arrived[...], hot[:, lanes]).astype(BF)

    def residual(g):
        line, size = groups[g]
        lanes = slice(line * n_pos, (line + size) * n_pos)
        model = mm(jac_t[...], obs_s[g % 2][:, : size * n_pos])
        copies[g][1].wait()
        own = jnp.concatenate([deps[line + k] for k in range(size)], axis=1)
        res = jnp.where(valid[:, lanes] > 0, model - own.astype(F32), 0.0)
        res_s[g % 2][:, : size * n_pos] = res.astype(BF)

    def weigh(g):
        line, size = groups[g]
        w_s[:, line * n_pos : (line + size) * n_pos] = mm(prec[...], res_s[g % 2][:, : size * n_pos])

    def scale(i):
        at = i * n_pos
        beside = w_s[:, at - n_pos : at] + w_s[:, at + n_pos : at + 2 * n_pos]
        val = inner * w_s[:, at : at + n_pos] - rf * beside
        sc_s[:, at : at + n_pos] = jnp.where(valid[:, at : at + n_pos] > 0, val, 0.0).astype(BF)

    outer = mm(prec[...], jnp.concatenate([first[...], last[...]], axis=1))
    w_s[:, :n_pos] = outer[:, :n_pos]
    w_s[:, total - n_pos :] = outer[:, n_pos:]
    done = 1
    count = len(groups)
    for t in range(count + 3):
        if t < count:
            gather(t)
        if 0 <= t - 1 < count:
            residual(t - 1)
        if 0 <= t - 2 < count:
            weigh(t - 2)
        if 0 <= t - 3 < count:
            line, size = groups[t - 3]
            stop = n_lines - 1 if t - 3 == count - 1 else line + size - 1
            while done < stop:
                scale(done)
                done += 1

    edges[:, : 2 * n_pos] = w_s[:, : 2 * n_pos]
    edges[:, 2 * n_pos :] = w_s[:, total - 2 * n_pos :]
    lanes = slice(n_pos, total - n_pos)
    step = min(256, n_slots)

    @pl.loop(0, n_slots // step)
    def _(q):
        at = pl.multiple_of(q * step, step)
        part[:, pl.ds(at, step)] = mm_nt(sc_s[:, lanes], hot[pl.ds(at, step), lanes])


def finish_kernel(rf, norm, inner, n_band, band, before, after, edges, slot, valid, part, jac, prec, wire):
    prof = jac.shape[0]
    n_slots = part.shape[1]
    n_pos = before.shape[1]
    total = slot.shape[1]
    outer = mm(prec[...], jnp.concatenate([before[...], after[...]], axis=1))
    ends = []
    for side, line_at, bound in ((0, 0, 0), (1, total - n_pos, n_band - 1)):
        own = edges[:, 3 * side * n_pos : (3 * side + 1) * n_pos]
        inside = edges[:, (1 + side) * n_pos : (2 + side) * n_pos]
        beyond = outer[:, side * n_pos : (side + 1) * n_pos]
        diag = jnp.where(band[0] == bound, norm, inner).astype(F32)
        val = diag * own - rf * (inside + beyond)
        ends.append(jnp.where(valid[:, line_at : line_at + n_pos] > 0, val, 0.0).astype(BF))
    scaled = jnp.concatenate(ends, axis=1)
    idx = jnp.concatenate([slot[:, 0:n_pos], slot[:, total - n_pos :]], axis=1)
    blocks = []
    step = n_slots // 4
    for c in range(4):
        row = lax.broadcasted_iota(jnp.int32, (step, 2 * n_pos), 0) + c * step
        hot = jnp.where(row == idx, 1.0, 0.0).astype(BF)
        sums = part[:, c * step : (c + 1) * step] + mm_nt(scaled, hot)
        high = sums.astype(BF)
        low = (sums - high.astype(F32)).astype(BF)
        blocks.append(mm(jac[...], high) + mm(jac[...], low))
    pack_wire(wire, blocks, prof)


def collect_kernel(wire, hot_in, grad, back, hot, out, sems):
    prof = back.shape[0]
    n_steps, step = out.shape[0], out.shape[2]
    copies = []
    for q in range(n_steps):
        rows = pl.ds(q * step, step)
        pair = (
            pltpu.make_async_copy(hot_in.at[rows], hot.at[rows], sems.at[0, q]),
            pltpu.make_async_copy(out.at[q], grad.at[:, rows], sems.at[1, q]),
        )
        pair[0].start()
        copies.append(pair)
    unpack_wire(wire, back, prof)
    for q in range(n_steps):
        copies[q][0].wait()
        out[q] = mm_nt(back[...], hot[q * step : (q + 1) * step, :])
        copies[q][1].start()
    for q in range(n_steps):
        copies[q][1].wait()


def call(body, outs, in_specs, limit, flops=0, scratch=(), out_specs=None):
    return pl.pallas_call(
        body,
        out_shape=outs,
        in_specs=in_specs,
        out_specs=out_specs or [VMEM] * len(outs),
        scratch_shapes=list(scratch),
        compiler_params=pltpu.CompilerParams(vmem_limit_bytes=int(limit * MIB)),
        cost_estimate=pl.CostEstimate(flops=flops, bytes_accessed=8 * MIB, transcendentals=0),
    )


def on_device(columns, departures, jacobian, chan_precision, send_rows, obs_slot, counts):
    decay = math.exp(-1.0 / corr_length)
    norm = 1.0 / (1.0 - decay * decay)
    rf, inner = decay * norm, (1.0 + decay * decay) * norm
    n_band = lax.axis_size("band")
    n_dev = n_band * lax.axis_size("lev")
    n_cols, prof = columns.shape
    _, n_lines, n_pos, n_chan = departures.shape
    total = n_lines * n_pos
    depth = send_rows.shape[2]
    n_slots = n_dev * depth
    sds = jax.ShapeDtypeStruct

    plan = send_rows[0].T
    jac_t = jacobian.T
    dep = departures[0].transpose(0, 2, 1)
    slots = obs_slot[0].reshape(1, total)
    slots = (slots % depth) * n_dev + slots // depth
    valid = jnp.arange(n_pos, dtype=jnp.int32)[None, :] < counts[0][:, None]
    valid = valid.astype(jnp.int32).reshape(1, total)

    wire_shape = sds((2, n_dev, WIRE), BF)

    def exchange(wire):
        sent = wire.transpose(1, 0, 2)
        got = lax.all_to_all(sent, ("band", "lev"), split_axis=0, concat_axis=0, tiled=True)
        return got.transpose(1, 0, 2)

    hot_shape = sds((n_cols, n_slots), BF)
    (wire,) = call(
        send_kernel,
        [wire_shape],
        [HBM, VMEM],
        62.9,
        2**31,
        scratch=[pltpu.VMEM((n_cols, n_slots), BF), pltpu.VMEM((prof, n_cols), BF), pltpu.SemaphoreType.DMA],
    )(columns.T, plan)
    got = exchange(wire)
    (hot,) = call(hot_kernel, [sds((n_slots, total), BF)], [VMEM], 60, 2**32)(slots)
    line_shape = sds((n_chan, n_pos), BF)
    arrived, first, last = call(
        edge_kernel,
        [sds((prof, n_slots), BF), line_shape, line_shape],
        [VMEM] * 3 + [HBM, VMEM],
        60,
        2**30,
        scratch=[pltpu.VMEM((2, n_chan, n_pos), BF), pltpu.SemaphoreType.DMA((2,))],
    )(got, slots, valid, dep, jac_t)
    ends = n_band - 1
    before = lax.ppermute(last, "band", [(i, i + 1) for i in range(ends)])
    after = lax.ppermute(first, "band", [(i + 1, i) for i in range(ends)])
    part, edges = call(
        functools.partial(main_kernel, rf, inner),
        [sds((n_chan, n_slots), F32), sds((n_chan, 4 * n_pos), F32)],
        [VMEM, HBM, VMEM, HBM] + [VMEM] * 4,
        60,
        2**34,
        scratch=[
            pltpu.VMEM((n_chan, total), F32),
            pltpu.VMEM((n_chan, total), BF),
            pltpu.VMEM((n_lines, n_chan, n_pos), BF),
            pltpu.VMEM((n_slots, total), BF),
            pltpu.SemaphoreType.DMA((2, n_lines)),
        ]
        + [pltpu.VMEM((prof, 4 * n_pos), BF)] * 2
        + [pltpu.VMEM((n_chan, 4 * n_pos), BF)] * 2,
    )(arrived, hot, valid, dep, jac_t, chan_precision, first, last)
    band = lax.axis_index("band").reshape(1)
    (wire,) = call(
        functools.partial(finish_kernel, rf, norm, inner, n_band),
        [wire_shape],
        [SMEM] + [VMEM] * 8,
        16,
        2**31,
    )(band, before, after, edges, slots, valid, part, jacobian, chan_precision)
    wire, late_plan = lax.optimization_barrier((wire, plan))
    back = exchange(wire)
    (hot_cols,) = call(hot_plan_kernel, [hot_shape], [VMEM], 60, 2**32)(late_plan)
    (grad,) = call(
        collect_kernel,
        [sds((prof, n_cols), F32)],
        [VMEM, HBM],
        61,
        2**31,
        scratch=[
            pltpu.VMEM((prof, n_slots), BF),
            pltpu.VMEM((n_cols, n_slots), BF),
            pltpu.VMEM((4, prof, n_cols // 4), F32),
            pltpu.SemaphoreType.DMA((2, 4)),
        ],
        out_specs=[HBM],
    )(back, hot_cols)
    return grad.T


def solution(mesh):
    placed = (
        P(("band", "lev"), None),
        P("lev", "band", None, None),
        P(),
        P(),
        P(("band", "lev"), None, None),
        P("lev", "band", None),
        P("lev", "band"),
    )
    return jax.shard_map(
        on_device, mesh=mesh, in_specs=placed, out_specs=P(("band", "lev"), None), check_vma=False
    )
```

time: 130 us -> 127 us (0.977)
  blocking collectives: 32.4 us -> 0 us
  waiting for transfers between devices: 20.3 us -> 33.9 us
  starting transfers between devices: 20 us -> 30.2 us
  Pallas kernels: 46.3 us -> 50.1 us
  local copies, waits for them, and re-layouts: 8.18 us -> 10.1 us
    all_to_all x1 -> x0, blocking collectives: 32.4 us -> none  [exchange(): lax.all_to_all(sent, ('band', 'lev'), split_axis=0, concat_axis=0, tiled=...]
    all_to_all x1 -> x2, waiting for transfers between devices: 20.3 us -> 33.9 us  [exchange(): lax.all_to_all(sent, ('band', 'lev'), split_axis=0, concat_axis=0, tiled=...]
    all_to_all x1 -> x2, starting transfers between devices: 15.6 us -> 25.6 us  [exchange(): lax.all_to_all(sent, ('band', 'lev'), split_axis=0, concat_axis=0, tiled=...]
    pallas_call x4 -> x6, Pallas kernels: 18.9 us -> 24.1 us  [the longest x1 5.44 us: on_device(): call(hot_kernel, [sds((n_slots, total), BF)], [VMEM], 60, 2 ** 32)(slots)]
    unnamed x7 -> x17, local copies, waits for them, and re-layouts: 0.99 us -> 4.02 us
  transfers between devices with their start and end apart: 3 -> 4, of which waited for: 1 -> 2; matrix products, arithmetic and copies ran while one was open for 2% -> 2% of each run, Pallas kernels for 21% -> 28%
where the time goes in v2:
time: 127 us; the launch traced here: 126 us
  Pallas kernels  50.1 us (39%)
  waiting for transfers between devices  33.9 us (27%)
  starting transfers between devices  30.2 us (24%)
  local copies, waits for them, and re-layouts  10.1 us (8%)
  other arithmetic  1.4 us (1%)
    all_to_all x2, waiting for transfers between devices, exchange(): lax.all_to_all(sent, ('band', 'lev'), split_axis=0, concat_axis=0, tiled=...  33.9 us
    pallas_call x1, Pallas kernels, on_device(): call(functools.partial(main_kernel, rf, inner), [sds((n_chan, n_slots), F...  26.1 us
    all_to_all x2, starting transfers between devices, exchange(): lax.all_to_all(sent, ('band', 'lev'), split_axis=0, concat_axis=0, tiled=...  25.6 us
    pallas_call x1, Pallas kernels, on_device(): call(hot_kernel, [sds((n_slots, total), BF)], [VMEM], 60, 2 ** 32)(slots)  5.44 us
    pallas_call x1, Pallas kernels, on_device(): call(collect_kernel, [sds((prof, n_cols), F32)], [VMEM, HBM], 61, 2 ** 31...  5.21 us
    pallas_call x1, Pallas kernels, on_device(): call(send_kernel, [wire_shape], [HBM, VMEM], 62.9, 2 ** 31, scratch=[pltp...  4.25 us
    transpose x2, local copies, waits for them, and re-layouts, exchange(): sent = wire.transpose(1, 0, 2)  4.22 us
    unnamed x17, local copies, waits for them, and re-layouts  4.02 us
  transfers between devices with their start and end apart: 4, of which 2 were waited for; matrix products, arithmetic and copies ran while one was open for 2% of the time, Pallas kernels for 28%

profile of v2, /device:TPU:1, one launch (start us, length us, event | category | flops | bytes accessed | tf_op | source)
XLA Modules:
  0.0 126.0 jit_solution(14481036779335509842)
XLA Ops:
  0.0 4.2 %shard_map.73 = bf16[2,256,640]{2,1,0:T(8,128)(2,1)} custom-call(bf16[274,2048]{1,0:T(8,128)(2,1)} %bitcast.34, s32[4,256]{1,0:T(4,128)} %bitcast.35), custom_call_target="tpu_custom_call" | custom-call | flops 2147483648 | bytes 8388608 | tf_op jit(solution)/shard_map/pallas_call | solution.py:274
  4.3 0.0 copy-start.7
  4.3 0.0 copy-start.6
  4.3 2.7 %copy.9 = bf16[256,2,640]{2,1,0:T(2,128)(2,1)} copy(bf16[256,2,640]{2,0,1:T(8,128)(2,1)} %bitcast.31) | data formatting | bytes 1310720 | tf_op jit(solution)/shard_map/transpose | solution.py:269
  7.0 15.6 %all-to-all-start = ((bf16[256,2,640]{2,1,0:T(2,128)(2,1)}), bf16[256,2,640]{2,1,0:T(2,128)(2,1)S(1)}, u32[]{:S(2)}, u32[]{:S(2)}) async-start(bf16[256,2,640]{2,1,0:T(2,128)(2,1)} %copy.9), calls=%async_computation | async-start | bytes 1310720 | tf_op jit(solution)/shard_map/all_to_all | solution.py:270
  22.7 0.7 fusion.2
  23.3 1.0 copy.11
  24.3 0.7 fusion.1.slot
  25.0 5.4 %shard_map.75.hot_in = bf16[1024,4096]{1,0:T(8,128)(2,1)} custom-call(s32[1,4096]{1,0:T(1,128)} %fusion.1.slot), custom_call_target="tpu_custom_call" | custom-call | flops 4294967296 | bytes 8388608 | tf_op jit(solution)/shard_map/pallas_call | solution.py:283
  30.5 14.8 %all-to-all-done = bf16[256,2,640]{2,1,0:T(2,128)(2,1)S(1)} async-done(((bf16[256,2,640]{2,1,0:T(2,128)(2,1)}), bf16[256,2,640]{2,1,0:T(2,128)(2,1)S(1)}, u32[]{:S(2)}, u32[]{:S(2)}) %all-to-all-start) | async-done | bytes 655392 | tf_op jit(solution)/shard_map/all_to_all | solution.py:270
  45.3 0.9 copy.17
  46.2 3.2 %shard_map.74 = (bf16[274,1024]{1,0:T(8,128)(2,1)}, bf16[616,128]{1,0:T(8,128)(2,1)}, bf16[616,128]{1,0:T(8,128)(2,1)}) custom-call(bf16[2,256,640]{2,1,0:T(8,128)(2,1)} %bitcast.27, s32[1,4096]{1,0:T(1,128)} %fusion.1.slot, s32[1,4096]{1,0:T(1,128)} %bitcast.22, bf16[32,616,128]{2,1,0:T(8,128)(2,1)} %bitcast.25, bf16[616,274]{1,0:T(8,128)(2,1)} %bitcast.28), custom_call_target="tpu_custom_call" | custom-call | flops 1073741824 | bytes 8388608 | tf_op jit(solution)/shard_map/pallas_call | solution.py:285
  49.4 2.4 %collective-permute-start = (bf16[616,128]{1,0:T(8,128)(2,1)}, bf16[616,128]{1,0:T(8,128)(2,1)S(1)}, u32[]{:S(2)}, u32[]{:S(2)}) collective-permute-start(bf16[616,128]{1,0:T(8,128)(2,1)} %get-tuple-element.12.last), channel_id=1, source_target_pairs={{0,4},{4,8},{8,12},{12,16},{16,20},{20,24},{24,28},{28,32},{32,36}... | collective-permute-start | bytes 473096 | tf_op jit(solution)/shard_map/ppermute | solution.py:294
  51.8 2.1 %collective-permute-start.1 = (bf16[616,128]{1,0:T(8,128)(2,1)}, bf16[616,128]{1,0:T(8,128)(2,1)S(1)}, u32[]{:S(2)}, u32[]{:S(2)}) collective-permute-start(bf16[616,128]{1,0:T(8,128)(2,1)} %get-tuple-element.13.first), channel_id=1, source_target_pairs={{4,0},{8,4},{12,8},{16,12},{20,16},{24,20},{28,24},{32,28},{36,32}... | collective-permute-start | bytes 473096 | tf_op jit(solution)/shard_map/ppermute | solution.py:295
  54.0 26.1 %shard_map.76 = (f32[616,1024]{1,0:T(8,128)}, f32[616,512]{1,0:T(8,128)}) custom-call(bf16[274,1024]{1,0:T(8,128)(2,1)} %get-tuple-element.14.arrived, bf16[1024,4096]{1,0:T(8,128)(2,1)} %shard_map.75.hot_in, s32[1,4096]{1,0:T(1,128)} %bitcast.23, bf16[32,616,128]{2,1,0:T(8,128)(2,1)} %bitcast.26, bf16[616,274]{1,0:T(8,128)(2,1)} %bitcast.29, ...), custom_call_target="tpu_custom_call" | custom-call | flops 17179869184 | bytes 8388608 | tf_op jit(solution)/shard_map/pallas_call | solution.py:296
  80.1 1.7 %copy-done.4 = f32[616,1024]{1,0:T(8,128)S(1)} copy-done((f32[616,1024]{1,0:T(8,128)S(1)}, f32[616,1024]{1,0:T(8,128)}, u32[]{:S(2)}) %copy-start.4) | copy-done | bytes 2523160
  81.8 1.3 %copy-done.5 = f32[616,512]{1,0:T(8,128)S(1)} copy-done((f32[616,512]{1,0:T(8,128)S(1)}, f32[616,512]{1,0:T(8,128)}, u32[]{:S(2)}) %copy-start.5) | copy-done | bytes 1261592
  83.1 2.4 %shard_map.77 = bf16[2,256,640]{2,1,0:T(8,128)(2,1)S(1)} custom-call(s32[1]{0:T(128)} %bitcast.band, bf16[616,128]{1,0:T(8,128)(2,1)S(1)} %collective-permute-done.before, bf16[616,128]{1,0:T(8,128)(2,1)S(1)} %collective-permute-done.1.after, f32[616,512]{1,0:T(8,128)S(1)} %copy-done.5, s32[1,4096]{1,0:T(1,128)S(1)} %copy-done.2, s32[1,4096]{1,0:T(1,128)S(1)} %bitcast.24, ...), custom_call_target="tpu_custom_call" | custom-call | flops 2147483648 | bytes 8388608 | tf_op jit(solution)/shard_map/pallas_call | solution.py:313
  85.5 1.5 %copy.12 = bf16[256,2,640]{2,1,0:T(2,128)(2,1)} copy(bf16[256,2,640]{2,0,1:T(8,128)(2,1)S(1)} %bitcast.21) | data formatting | bytes 1310720 | tf_op jit(solution)/shard_map/transpose | solution.py:269
  87.1 10.0 %all-to-all-start.1 = ((bf16[256,2,640]{2,1,0:T(2,128)(2,1)}), bf16[256,2,640]{2,1,0:T(2,128)(2,1)S(1)}, u32[]{:S(2)}, u32[]{:S(2)}) async-start(bf16[256,2,640]{2,1,0:T(2,128)(2,1)} %copy.12), calls=%async_computation.1 | async-start | bytes 1310720 | tf_op jit(solution)/shard_map/all_to_all | solution.py:270
  97.0 3.6 %shard_map.78.hot_in = bf16[2048,1024]{1,0:T(8,128)(2,1)} custom-call(s32[4,256]{1,0:T(4,128)} %bitcast.36), custom_call_target="tpu_custom_call" | custom-call | flops 4294967296 | bytes 8388608 | tf_op jit(solution)/shard_map/pallas_call | solution.py:322
  100.6 19.1 %all-to-all-done.1 = bf16[256,2,640]{2,1,0:T(2,128)(2,1)S(1)} async-done(((bf16[256,2,640]{2,1,0:T(2,128)(2,1)}), bf16[256,2,640]{2,1,0:T(2,128)(2,1)S(1)}, u32[]{:S(2)}, u32[]{:S(2)}) %all-to-all-start.1) | async-done | bytes 655392 | tf_op jit(solution)/shard_map/all_to_all | solution.py:270
  119.7 0.9 copy.16
  120.6 5.2 %shard_map.79 = f32[274,2048]{1,0:T(8,128)} custom-call(bf16[2,256,640]{2,1,0:T(8,128)(2,1)} %bitcast.30, bf16[2048,1024]{1,0:T(8,128)(2,1)} %shard_map.78.hot_in), custom_call_target="tpu_custom_call" | custom-call | flops 2147483648 | bytes 8388608 | tf_op jit(solution)/shard_map/pallas_call | solution.py:323
  (14 shorter events, 0.0 us)
Async XLA Ops:
  4.3 18.4 %copy-start.7 = (s32[1,32]{1,0:T(1,128)S(1)}, s32[1,32]{1,0:T(1,128)}, u32[]{:S(2)}) copy-start(s32[1,32]{1,0:T(1,128)} %param.13) | copy-start | bytes 388
  4.3 19.1 %copy-start = (bf16[274,616]{1,0:T(8,128)(2,1)S(1)}, bf16[274,616]{1,0:T(8,128)(2,1)}, u32[]{:S(2)}) copy-start(bf16[274,616]{1,0:T(8,128)(2,1)} %jac.1) | copy-start | bytes 1012708
  4.3 20.0 %copy-start.6 = (s32[1,32,128]{2,1,0:T(8,128)S(1)}, s32[1,32,128]{2,1,0:T(8,128)}, u32[]{:S(2)}) copy-start(s32[1,32,128]{2,1,0:T(8,128)} %param.12) | copy-start | bytes 49156
  7.0 38.3 %all-to-all-start = ((bf16[256,2,640]{2,1,0:T(2,128)(2,1)}), bf16[256,2,640]{2,1,0:T(2,128)(2,1)S(1)}, u32[]{:S(2)}, u32[]{:S(2)}) async-start(bf16[256,2,640]{2,1,0:T(2,128)(2,1)} %copy.9), calls=%async_computation | async-start | bytes 1310720 | tf_op jit(solution)/shard_map/all_to_all | solution.py:270
  49.4 30.7 %collective-permute-start = (bf16[616,128]{1,0:T(8,128)(2,1)}, bf16[616,128]{1,0:T(8,128)(2,1)S(1)}, u32[]{:S(2)}, u32[]{:S(2)}) collective-permute-start(bf16[616,128]{1,0:T(8,128)(2,1)} %get-tuple-element.12.last), channel_id=1, source_target_pairs={{0,4},{4,8},{8,12},{12,16},{16,20},{20,24},{24,28},{28,32},{32,36}... | collective-permute-start | bytes 473096 | tf_op jit(solution)/shard_map/ppermute | solution.py:294
  51.8 28.2 %collective-permute-start.1 = (bf16[616,128]{1,0:T(8,128)(2,1)}, bf16[616,128]{1,0:T(8,128)(2,1)S(1)}, u32[]{:S(2)}, u32[]{:S(2)}) collective-permute-start(bf16[616,128]{1,0:T(8,128)(2,1)} %get-tuple-element.13.first), channel_id=1, source_target_pairs={{4,0},{8,4},{12,8},{16,12},{20,16},{24,20},{28,24},{32,28},{36,32}... | collective-permute-start | bytes 473096 | tf_op jit(solution)/shard_map/ppermute | solution.py:295
  53.9 26.1 %copy-start.1 = (s32[32,128]{1,0:T(8,128)S(1)}, s32[32,128]{1,0:T(8,128)}, u32[]{:S(2)}) copy-start(s32[32,128]{1,0:T(8,128)} %fusion.2) | copy-start | bytes 49156
  53.9 26.1 %copy-start.2 = (s32[1,4096]{1,0:T(1,128)S(1)}, s32[1,4096]{1,0:T(1,128)}, u32[]{:S(2)}) copy-start(s32[1,4096]{1,0:T(1,128)} %fusion.1.slot) | copy-start | bytes 49156
  54.0 26.1 %copy-start.3 = (bf16[616,616]{1,0:T(8,128)(2,1)S(1)}, bf16[616,616]{1,0:T(8,128)(2,1)}, u32[]{:S(2)}) copy-start(bf16[616,616]{1,0:T(8,128)(2,1)} %prec.3) | copy-start | bytes 2276740
  80.1 1.7 %copy-start.4 = (f32[616,1024]{1,0:T(8,128)S(1)}, f32[616,1024]{1,0:T(8,128)}, u32[]{:S(2)}) copy-start(f32[616,1024]{1,0:T(8,128)} %get-tuple-element.16.part) | copy-start | bytes 7569412
  81.8 1.3 %copy-start.5 = (f32[616,512]{1,0:T(8,128)S(1)}, f32[616,512]{1,0:T(8,128)}, u32[]{:S(2)}) copy-start(f32[616,512]{1,0:T(8,128)} %get-tuple-element.15.edges) | copy-start | bytes 3784708
  87.1 32.6 %all-to-all-start.1 = ((bf16[256,2,640]{2,1,0:T(2,128)(2,1)}), bf16[256,2,640]{2,1,0:T(2,128)(2,1)S(1)}, u32[]{:S(2)}, u32[]{:S(2)}) async-start(bf16[256,2,640]{2,1,0:T(2,128)(2,1)} %copy.12), calls=%async_computation.1 | async-start | bytes 1310720 | tf_op jit(solution)/shard_map/all_to_all | solution.py:270

commit v3 on v2

v3 whole, which is shorter than its diff:
```python
import functools
import math

import jax
import jax.numpy as jnp
from jax import lax
from jax.experimental import pallas as pl
from jax.experimental.pallas import tpu as pltpu
from jax.sharding import PartitionSpec as P

corr_length = 2.0
BF, F32 = jnp.bfloat16, jnp.float32
NT = (((1,), (1,)), ((), ()))
VMEM = pl.BlockSpec(memory_space=pltpu.VMEM)
SMEM = pl.BlockSpec(memory_space=pltpu.SMEM)
HBM = pl.BlockSpec(memory_space=pltpu.HBM)
MIB = 1024 * 1024
LIMITS = (16, 60, 60, 60, 16)
GROUP = 4
MAIN, TAIL_AT, TAIL_STEP, WIRE = 256, 512, 64, 640


def mm(a, b):
    return jnp.dot(a, b, preferred_element_type=F32)


def mm_nt(a, b):
    return lax.dot_general(a, b, NT, preferred_element_type=F32)


def write_hot(out, first_col, idx, base=0):
    n = idx.shape[1]
    row = lax.broadcasted_iota(jnp.int32, (16, n), 0) + base
    gap = (jnp.broadcast_to(idx, (16, n)) - row).astype(jnp.int16)
    one, zero = jnp.ones((16, n), BF), jnp.zeros((16, n), BF)
    for r in range(0, out.shape[0], 16):
        out[r : r + 16, pl.ds(first_col, n)] = jnp.where(gap == jnp.int16(r), one, zero)


def pack_wire(wire, r, blocks, prof):
    n = blocks[0].shape[1]
    tails = []
    for par, block in enumerate(blocks):
        wire[r, :, par * MAIN : (par + 1) * MAIN] = block[:MAIN].T.astype(BF)
        fill = jnp.zeros((TAIL_STEP - (prof - MAIN), n), block.dtype)
        tails.extend([block[MAIN:], fill])
    wire[r, :, TAIL_AT:] = jnp.concatenate(tails, axis=0).T.astype(BF)


def unpack_wire(wire, out, prof):
    n = wire.shape[1]
    for r in range(2):
        turned = wire[r].astype(F32).T.astype(BF)
        for par in range(2):
            c = 2 * r + par
            out[0:MAIN, c * n : (c + 1) * n] = turned[par * MAIN : (par + 1) * MAIN]
            at = TAIL_AT + par * TAIL_STEP
            out[MAIN:prof, c * n : (c + 1) * n] = turned[at : at + prof - MAIN]


def send_kernel(cols_in, plan, wire, hot, cols, sem):
    prof, n_cols = cols.shape
    copy = pltpu.make_async_copy(cols_in, cols, sem)
    copy.start()
    n = plan.shape[1]
    for c in range(4):
        write_hot(hot, c * n, plan[c : c + 1, :])
    copy.wait()
    for r in range(2):
        blocks = [mm(cols[...], hot[:, c * n : (c + 1) * n]) for c in (2 * r, 2 * r + 1)]
        pack_wire(wire, r, blocks, prof)


def hot_kernel(slot, hot):
    width = 512

    @pl.loop(0, hot.shape[1] // width)
    def _(j):
        at = pl.multiple_of(j * width, width)
        write_hot(hot, at, slot[:, pl.ds(at, width)])


def edge_kernel(wire, slot, valid, dep, jac_t, arrived, first, last, deps, hot, sems):
    copies = [
        pltpu.make_async_copy(dep.at[line], deps.at[k], sems.at[k]) for k, line in enumerate((0, dep.shape[0] - 1))
    ]
    for copy in copies:
        copy.start()
    prof = arrived.shape[0]
    unpack_wire(wire, arrived, prof)
    n_pos = dep.shape[2]
    end = slot.shape[1] - n_pos
    write_hot(hot, 0, jnp.concatenate([slot[:, :n_pos], slot[:, end:]], axis=1))
    obs = mm(arrived[...], hot[...]).astype(BF)
    model = mm(jac_t[...], obs)
    for k, at, out in ((0, 0, first), (1, end, last)):
        copies[k].wait()
        res = model[:, k * n_pos : (k + 1) * n_pos] - deps[k].astype(F32)
        out[...] = jnp.where(valid[:, at : at + n_pos] > 0, res, 0.0).astype(BF)


def main_kernel(rf, inner, arrived_in, hot_in, valid, dep, jac_in, prec_in, part_out, edges_out, *scratch):
    arrived, jac_t, prec, deps, hot, obs_s, res_s, w_s, sc_s, part, in_sem, group_sem, out_sem = scratch
    n_slots = arrived.shape[1]
    n_lines, n_chan, n_pos = dep.shape
    total = n_lines * n_pos
    size = GROUP
    width = size * n_pos
    count = n_lines // size

    def hot_copy(g):
        lanes = pl.ds(pl.multiple_of(g * width, width), width)
        return pltpu.make_async_copy(hot_in.at[:, lanes], hot.at[:, lanes], group_sem.at[0, g])

    def dep_copy(g):
        span = pl.ds(g * size, size)
        return pltpu.make_async_copy(dep.at[span], deps.at[span], group_sem.at[1, g])

    whole = [
        pltpu.make_async_copy(src, dst, in_sem.at[k])
        for k, (src, dst) in enumerate(((arrived_in, arrived), (jac_in, jac_t), (prec_in, prec)))
    ]
    for copy in whole:
        copy.start()
    for g in range(count):
        hot_copy(g).start()
        dep_copy(g).start()
    for copy in whole:
        copy.wait()

    @pl.loop(0, count)
    def _(g):
        hot_copy(g).wait()
        dep_copy(g).wait()
        lanes = pl.ds(pl.multiple_of(g * width, width), width)
        obs_s[...] = mm(arrived[...], hot[:, lanes]).astype(BF)
        model = mm(jac_t[...], obs_s[...])
        own = jnp.concatenate([deps[g * size + k] for k in range(size)], axis=1)
        res_s[...] = jnp.where(valid[:, lanes] > 0, model - own.astype(F32), 0.0).astype(BF)
        w_s[:, lanes] = rf * mm(prec[...], res_s[...])

    sides = [
        pltpu.make_async_copy(w_s.at[:, pl.ds(at, 2 * n_pos)], edges_out.at[:, pl.ds(to, 2 * n_pos)], out_sem.at[4 + k])
        for k, (at, to) in enumerate(((0, 0), (total - 2 * n_pos, 2 * n_pos)))
    ]
    for copy in sides:
        copy.start()

    def scale(rows):
        before, here = w_s[rows, 0:n_pos], w_s[rows, n_pos : 2 * n_pos]
        for i in range(1, n_lines - 1):
            after = w_s[rows, (i + 1) * n_pos : (i + 2) * n_pos]
            sc_s[rows, i * n_pos : (i + 1) * n_pos] = ((inner / rf) * here - (before + after)).astype(BF)
            before, here = here, after

    @pl.loop(0, n_chan // 16)
    def _(c):
        scale(pl.ds(pl.multiple_of(c * 16, 16), 16))

    if n_chan % 16:
        scale(pl.ds(n_chan // 16 * 16, n_chan % 16))

    inside = slice(n_pos, total - n_pos)
    step = n_slots // 4

    def part_copy(q):
        lanes = pl.ds(pl.multiple_of(q * step, step), step)
        return pltpu.make_async_copy(part.at[:, lanes], part_out.at[:, lanes], out_sem.at[q])

    @pl.loop(0, 4)
    def _(q):
        at = pl.multiple_of(q * step, step)
        part[:, pl.ds(at, step)] = mm_nt(sc_s[:, inside], hot[pl.ds(at, step), inside])
        part_copy(q).start()

    for copy in sides:
        copy.wait()
    for q in range(4):
        part_copy(q).wait()


def finish_kernel(rf, norm, inner, n_band, band, before, after, edges_in, slot, part_in, jac, prec, wire, *scratch):
    edges, part, sems = scratch
    prof = jac.shape[0]
    n_slots = part.shape[1]
    n_pos = before.shape[1]
    total = slot.shape[1]
    step = n_slots // 4
    copies = [pltpu.make_async_copy(edges_in, edges, sems.at[4])]
    for c in range(4):
        lanes = pl.ds(c * step, step)
        copies.append(pltpu.make_async_copy(part_in.at[:, lanes], part.at[:, lanes], sems.at[c]))
    for copy in copies:
        copy.start()
    outer = rf * mm(prec[...], jnp.concatenate([before[...], after[...]], axis=1))
    copies[0].wait()
    ends = []
    for side, bound in ((0, 0), (1, n_band - 1)):
        own = edges[:, 3 * side * n_pos : (3 * side + 1) * n_pos]
        inside = edges[:, (1 + side) * n_pos : (2 + side) * n_pos]
        beyond = outer[:, side * n_pos : (side + 1) * n_pos]
        ratio = jnp.where(band[0] == bound, norm / rf, inner / rf).astype(F32)
        ends.append((ratio * own - (inside + beyond)).astype(BF))
    scaled = jnp.concatenate(ends, axis=1)
    idx = jnp.concatenate([slot[:, 0:n_pos], slot[:, total - n_pos :]], axis=1)
    for copy in copies[1:]:
        copy.wait()
    for r in range(2):
        blocks = []
        for c in (2 * r, 2 * r + 1):
            row = lax.broadcasted_iota(jnp.int32, (step, 2 * n_pos), 0) + c * step
            hot = jnp.where(row == idx, 1.0, 0.0).astype(BF)
            sums = part[:, c * step : (c + 1) * step] + mm_nt(scaled, hot)
            high = sums.astype(BF)
            low = (sums - high.astype(F32)).astype(BF)
            blocks.append(mm(jac[...], high) + mm(jac[...], low))
        pack_wire(wire, r, blocks, prof)


def collect_kernel(wire, plan, grad, back, hot, out, sems):
    prof = back.shape[0]
    n_steps, step = out.shape[0], out.shape[2]
    n = plan.shape[1]
    unpack_wire(wire, back, prof)
    copies = []
    for q in range(n_steps):
        for c in range(4):
            write_hot(hot.at[q], c * n, plan[c : c + 1, :], q * step)
        out[q] = mm_nt(back[...], hot[q])
        copies.append(pltpu.make_async_copy(out.at[q], grad.at[:, pl.ds(q * step, step)], sems.at[q]))
        copies[q].start()
    for copy in copies:
        copy.wait()


def call(body, outs, in_specs, limit, flops=0, scratch=(), out_specs=None):
    return pl.pallas_call(
        body,
        out_shape=outs,
        in_specs=in_specs,
        out_specs=out_specs or [VMEM] * len(outs),
        scratch_shapes=list(scratch),
        compiler_params=pltpu.CompilerParams(vmem_limit_bytes=int(limit * MIB)),
        cost_estimate=pl.CostEstimate(flops=flops, bytes_accessed=8 * MIB, transcendentals=0),
    )


def on_device(columns, departures, jacobian, chan_precision, send_rows, obs_slot, counts):
    decay = math.exp(-1.0 / corr_length)
    norm = 1.0 / (1.0 - decay * decay)
    rf, inner = decay * norm, (1.0 + decay * decay) * norm
    n_band = lax.axis_size("band")
    n_dev = n_band * lax.axis_size("lev")
    n_cols, prof = columns.shape
    _, n_lines, n_pos, n_chan = departures.shape
    total = n_lines * n_pos
    depth = send_rows.shape[2]
    n_slots = n_dev * depth
    sds = jax.ShapeDtypeStruct

    plan = send_rows[0].T
    jac_t = jacobian.T
    dep = departures[0].transpose(0, 2, 1)
    valid = jnp.arange(n_pos, dtype=jnp.int32)[None, :] < counts[0][:, None]
    slots = (obs_slot[0] % depth) * n_dev + obs_slot[0] // depth
    slots = jnp.where(valid, slots, -1).reshape(1, total)
    valid = valid.astype(jnp.int32).reshape(1, total)

    wire_shape = sds((2, n_dev, WIRE), BF)

    def exchange(wire):
        sent = wire.transpose(1, 0, 2)
        got = lax.all_to_all(sent, ("band", "lev"), split_axis=0, concat_axis=0, tiled=True)
        return got.transpose(1, 0, 2)

    dma = pltpu.SemaphoreType.DMA
    vm = pltpu.VMEM
    (wire,) = call(
        send_kernel,
        [wire_shape],
        [HBM, VMEM],
        LIMITS[0],
        2**31,
        scratch=[vm((n_cols, n_slots), BF), vm((prof, n_cols), BF), dma],
    )(columns.T, plan)
    got = exchange(wire)
    (hot,) = call(hot_kernel, [sds((n_slots, total), BF)], [VMEM], 60, 2**32)(slots)
    line_shape = sds((n_chan, n_pos), BF)
    arrived, first, last = call(
        edge_kernel,
        [sds((prof, n_slots), BF), line_shape, line_shape],
        [VMEM] * 3 + [HBM, VMEM],
        LIMITS[1],
        2**30,
        scratch=[vm((2, n_chan, n_pos), BF), vm((n_slots, 2 * n_pos), BF), dma((2,))],
    )(got, slots, valid, dep, jac_t)
    ends = n_band - 1
    before = lax.ppermute(last, "band", [(i, i + 1) for i in range(ends)])
    after = lax.ppermute(first, "band", [(i + 1, i) for i in range(ends)])
    part, edges = call(
        functools.partial(main_kernel, rf, inner),
        [sds((n_chan, n_slots), F32), sds((n_chan, 4 * n_pos), F32)],
        [HBM, HBM, VMEM, HBM, HBM, HBM],
        LIMITS[2],
        2**34,
        scratch=[
            vm((prof, n_slots), BF),
            vm((n_chan, prof), BF),
            vm((n_chan, n_chan), BF),
            vm((n_lines, n_chan, n_pos), BF),
            vm((n_slots, total), BF),
            vm((prof, GROUP * n_pos), BF),
            vm((n_chan, GROUP * n_pos), BF),
            vm((n_chan, total), F32),
            vm((n_chan, total), BF),
            vm((n_chan, n_slots), F32),
            dma((3,)),
            dma((2, n_lines // GROUP)),
            dma((6,)),
        ],
        out_specs=[HBM] * 2,
    )(arrived, hot, valid, dep, jac_t, chan_precision)
    band = lax.axis_index("band").reshape(1)
    (wire,) = call(
        functools.partial(finish_kernel, rf, norm, inner, n_band),
        [wire_shape],
        [SMEM, VMEM, VMEM, HBM, VMEM, HBM, VMEM, VMEM],
        LIMITS[3],
        2**31,
        scratch=[vm((n_chan, 4 * n_pos), F32), vm((n_chan, n_slots), F32), dma((5,))],
    )(band, before, after, edges, slots, part, jacobian, chan_precision)
    back = exchange(wire)
    (grad,) = call(
        collect_kernel,
        [sds((prof, n_cols), F32)],
        [VMEM, VMEM],
        LIMITS[4],
        2**31,
        scratch=[
            vm((prof, n_slots), BF),
            vm((4, n_cols // 4, n_slots), BF),
            vm((4, prof, n_cols // 4), F32),
            dma((4,)),
        ],
        out_specs=[HBM],
    )(back, plan)
    return grad.T


def solution(mesh):
    placed = (
        P(("band", "lev"), None),
        P("lev", "band", None, None),
        P(),
        P(),
        P(("band", "lev"), None, None),
        P("lev", "band", None),
        P("lev", "band"),
    )
    return jax.shard_map(
        on_device, mesh=mesh, in_specs=placed, out_specs=P(("band", "lev"), None), check_vma=False
    )
```

time: 127 us -> 122 us (0.961)
  blocking collectives: 0 us -> 32.5 us
  waiting for transfers between devices: 33.9 us -> 15.3 us
  starting transfers between devices: 30.2 us -> 20 us
  Pallas kernels: 50.1 us -> 44.7 us
  local copies, waits for them, and re-layouts: 10.1 us -> 7.92 us
    all_to_all x0 -> x1, blocking collectives: none -> 32.5 us  [exchange(): lax.all_to_all(sent, ('band', 'lev'), split_axis=0, concat_axis=0, tiled=...]
    all_to_all x2 -> x1, waiting for transfers between devices: 33.9 us -> 15.3 us  [exchange(): lax.all_to_all(sent, ('band', 'lev'), split_axis=0, concat_axis=0, tiled=...]
    all_to_all x2 -> x1, starting transfers between devices: 25.6 us -> 15.6 us  [exchange(): lax.all_to_all(sent, ('band', 'lev'), split_axis=0, concat_axis=0, tiled=...]
    pallas_call x3 -> x2, Pallas kernels: 13 us -> 4.24 us  [the longest x1 2.29 us: on_device(): call(collect_kernel, [sds((prof, n_cols), F32)], [VMEM, VMEM], LIMITS[4],...]
    pallas_call x1, Pallas kernels: 2.44 us -> 6.34 us  [on_device(): call(functools.partial(finish_kernel, rf, norm, inner, n_band), [wire_sha...]
  transfers between devices with their start and end apart: 4 -> 3, of which waited for: 2 -> 1; matrix products, arithmetic and copies ran while one was open for 2% -> 2% of each run, Pallas kernels for 28% -> 25%
where the time goes in v3:
time: 122 us
  Pallas kernels  44.7 us (37%)
  blocking collectives  32.5 us (27%)
  starting transfers between devices  20 us (16%)
  waiting for transfers between devices  15.3 us (13%)
  local copies, waits for them, and re-layouts  7.92 us (6%)
  other arithmetic  1.44 us (1%)
    all_to_all x1, blocking collectives, exchange(): lax.all_to_all(sent, ('band', 'lev'), split_axis=0, concat_axis=0, tiled=...  32.5 us
    pallas_call x1, Pallas kernels, on_device(): call(functools.partial(main_kernel, rf, inner), [sds((n_chan, n_slots), F...  26.1 us
    all_to_all x1, starting transfers between devices, exchange(): lax.all_to_all(sent, ('band', 'lev'), split_axis=0, concat_axis=0, tiled=...  15.6 us
    all_to_all x1, waiting for transfers between devices, exchange(): lax.all_to_all(sent, ('band', 'lev'), split_axis=0, concat_axis=0, tiled=...  15.3 us
    pallas_call x1, Pallas kernels, on_device(): call(functools.partial(finish_kernel, rf, norm, inner, n_band), [wire_sha...  6.34 us
    pallas_call x1, Pallas kernels, on_device(): call(hot_kernel, [sds((n_slots, total), BF)], [VMEM], 60, 2 ** 32)(slots)  4.94 us
    unnamed x17, local copies, waits for them, and re-layouts  3.65 us
    transpose x2, local copies, waits for them, and re-layouts, exchange(): sent = wire.transpose(1, 0, 2)  3.28 us
  transfers between devices with their start and end apart: 3, of which 1 were waited for; matrix products, arithmetic and copies ran while one was open for 2% of the time, Pallas kernels for 25%

profile of v3, /device:TPU:1, one launch (start us, length us, event | category | flops | bytes accessed | tf_op | source)
XLA Modules:
  0.0 122.0 jit_solution(12730881733958164752)
XLA Ops:
  0.0 1.3 %copy-done = bf16[2048,274]{0,1:T(8,128)(2,1)S(1)} copy-done((bf16[2048,274]{0,1:T(8,128)(2,1)S(1)}, bf16[2048,274]{0,1:T(8,128)(2,1)}, u32[]{:S(2)}) %copy-start) | copy-done | bytes 1122328
  1.3 0.7 copy-done.1
  1.9 1.9 %shard_map.73 = bf16[2,256,640]{2,1,0:T(8,128)(2,1)S(1)} custom-call(bf16[274,2048]{1,0:T(8,128)(2,1)S(1)} %bitcast.28, s32[4,256]{1,0:T(4,128)S(1)} %bitcast.29), custom_call_target="tpu_custom_call" | custom-call | flops 2147483648 | bytes 8388608 | tf_op jit(solution)/shard_map/pallas_call | solution.py:278
  3.9 0.0 copy-start.5
  3.9 1.5 %copy.9 = bf16[256,2,640]{2,1,0:T(2,128)(2,1)} copy(bf16[256,2,640]{2,0,1:T(8,128)(2,1)S(1)} %bitcast.27) | data formatting | bytes 1310720 | tf_op jit(solution)/shard_map/transpose | solution.py:272
  5.5 15.6 %all-to-all-start = ((bf16[256,2,640]{2,1,0:T(2,128)(2,1)}), bf16[256,2,640]{2,1,0:T(2,128)(2,1)S(1)}, u32[]{:S(2)}, u32[]{:S(2)}) async-start(bf16[256,2,640]{2,1,0:T(2,128)(2,1)} %copy.9), calls=%async_computation | async-start | bytes 1310720 | tf_op jit(solution)/shard_map/all_to_all | solution.py:273
  21.1 0.1 fusion.2
  21.2 0.7 bitcast_select_fusion.slot
  21.9 1.0 copy.11
  22.9 4.9 %shard_map.75.hot_in = bf16[1024,4096]{1,0:T(8,128)(2,1)} custom-call(s32[1,4096]{1,0:T(1,128)} %bitcast_select_fusion.slot), custom_call_target="tpu_custom_call" | custom-call | flops 4294967296 | bytes 8388608 | tf_op jit(solution)/shard_map/pallas_call | solution.py:287
  27.8 0.6 bitcast_convert_fusion.valid
  28.5 15.3 %all-to-all-done = bf16[256,2,640]{2,1,0:T(2,128)(2,1)S(1)} async-done(((bf16[256,2,640]{2,1,0:T(2,128)(2,1)}), bf16[256,2,640]{2,1,0:T(2,128)(2,1)S(1)}, u32[]{:S(2)}, u32[]{:S(2)}) %all-to-all-start) | async-done | bytes 655392 | tf_op jit(solution)/shard_map/all_to_all | solution.py:273
  43.8 0.9 copy.20
  44.7 3.2 %shard_map.74 = (bf16[274,1024]{1,0:T(8,128)(2,1)}, bf16[616,128]{1,0:T(8,128)(2,1)}, bf16[616,128]{1,0:T(8,128)(2,1)}) custom-call(bf16[2,256,640]{2,1,0:T(8,128)(2,1)} %bitcast.33, s32[1,4096]{1,0:T(1,128)} %bitcast_select_fusion.slot, s32[1,4096]{1,0:T(1,128)} %bitcast_convert_fusion.valid, bf16[32,616,128]{2,1,0:T(8,128)(2,1)} %bitcast.31, ...), custom_call_target="tpu_custom_call" | custom-call | flops 1073741824 | bytes 8388608 | tf_op jit(solution)/shard_map/pallas_call | solution.py:289
  47.8 2.4 %collective-permute-start = (bf16[616,128]{1,0:T(8,128)(2,1)}, bf16[616,128]{1,0:T(8,128)(2,1)S(1)}, u32[]{:S(2)}, u32[]{:S(2)}) collective-permute-start(bf16[616,128]{1,0:T(8,128)(2,1)} %get-tuple-element.10), channel_id=1, source_target_pairs={{0,4},{4,8},{8,12},{12,16},{16,20},{20,24},{24,28},{28,32},{32,36}... | collective-permute-start | bytes 473096 | tf_op jit(solution)/shard_map/ppermute | solution.py:298
  50.3 1.9 %collective-permute-start.1 = (bf16[616,128]{1,0:T(8,128)(2,1)}, bf16[616,128]{1,0:T(8,128)(2,1)S(1)}, u32[]{:S(2)}, u32[]{:S(2)}) collective-permute-start(bf16[616,128]{1,0:T(8,128)(2,1)} %get-tuple-element.11), channel_id=1, source_target_pairs={{4,0},{8,4},{12,8},{16,12},{20,16},{24,20},{28,24},{32,28},{36,32}... | collective-permute-start | bytes 473096 | tf_op jit(solution)/shard_map/ppermute | solution.py:299
  52.2 26.1 %shard_map.76 = (f32[616,1024]{1,0:T(8,128)}, f32[616,512]{1,0:T(8,128)}) custom-call(bf16[274,1024]{1,0:T(8,128)(2,1)} %get-tuple-element.12.arrived_in, bf16[1024,4096]{1,0:T(8,128)(2,1)} %shard_map.75.hot_in, s32[1,4096]{1,0:T(1,128)} %bitcast_convert_fusion.valid, bf16[32,616,128]{2,1,0:T(8,128)(2,1)} %bitcast.32, bf16[616,274]{1,0:T(8,128)(2,1)} %bitcast.35, ...), custom_call_target="tpu_custom_call" | custom-call | flops 17179869184 | bytes 8388608 | tf_op jit(solution)/shard_map/pallas_call | solution.py:300
  78.3 0.6 copy-done.6
  78.9 0.1 copy-done.7
  79.0 6.3 %shard_map.77 = bf16[2,256,640]{2,1,0:T(8,128)(2,1)} custom-call(s32[1]{0:T(128)} %bitcast.band, bf16[616,128]{1,0:T(8,128)(2,1)} %copy-done.6, bf16[616,128]{1,0:T(8,128)(2,1)} %copy-done.7, f32[616,512]{1,0:T(8,128)} %get-tuple-element.13.edges_in, s32[1,4096]{1,0:T(1,128)} %bitcast_select_fusion.slot, f32[616,1024]{1,0:T(8,128)} %get-tuple-element.14.part_in, ...), custom_call_target="tpu_custom_call" | custom-call | flops 2147483648 | bytes 8388608 | tf_op jit(solution)/shard_map/pallas_call | solution.py:324
  85.4 1.8 %copy.12 = bf16[256,2,640]{2,1,0:T(2,128)(2,1)S(1)} copy(bf16[256,2,640]{2,0,1:T(8,128)(2,1)} %bitcast.36) | data formatting | bytes 1310720 | tf_op jit(solution)/shard_map/transpose | solution.py:272
  87.1 32.5 %all_to_all.10 = bf16[256,2,640]{2,1,0:T(2,128)(2,1)S(1)} all-to-all(bf16[256,2,640]{2,1,0:T(2,128)(2,1)S(1)} %copy.12), channel_id=1, replica_groups=mesh['band'=64,'lev'=4] {'band','lev'}, dimensions={0} | all-to-all | bytes 1310720 | tf_op jit(solution)/shard_map/all_to_all | solution.py:273
  119.6 0.1 copy.19
  119.7 2.3 %shard_map.78 = f32[274,2048]{1,0:T(8,128)} custom-call(bf16[2,256,640]{2,1,0:T(8,128)(2,1)S(1)} %bitcast.26, s32[4,256]{1,0:T(4,128)S(1)} %bitcast.30), custom_call_target="tpu_custom_call" | custom-call | flops 2147483648 | bytes 8388608 | tf_op jit(solution)/shard_map/pallas_call | solution.py:333
  (13 shorter events, 0.0 us)
Async XLA Ops:
  0.0 1.3 %copy-start = (bf16[2048,274]{0,1:T(8,128)(2,1)S(1)}, bf16[2048,274]{0,1:T(8,128)(2,1)}, u32[]{:S(2)}) copy-start(bf16[2048,274]{0,1:T(8,128)(2,1)} %param.7) | copy-start | bytes 3366916
  1.3 0.7 copy-start.1
  3.9 17.2 %copy-start.5 = (s32[1,32]{1,0:T(1,128)S(1)}, s32[1,32]{1,0:T(1,128)}, u32[]{:S(2)}) copy-start(s32[1,32]{1,0:T(1,128)} %param.13) | copy-start | bytes 388
  3.9 17.3 %copy-start.4 = (s32[1,32,128]{2,1,0:T(8,128)S(1)}, s32[1,32,128]{2,1,0:T(8,128)}, u32[]{:S(2)}) copy-start(s32[1,32,128]{2,1,0:T(8,128)} %param.12) | copy-start | bytes 49156
  3.9 18.0 %copy-start.3 = (bf16[274,616]{1,0:T(8,128)(2,1)S(1)}, bf16[274,616]{1,0:T(8,128)(2,1)}, u32[]{:S(2)}) copy-start(bf16[274,616]{1,0:T(8,128)(2,1)} %jac.1) | copy-start | bytes 1012708
  5.5 38.3 %all-to-all-start = ((bf16[256,2,640]{2,1,0:T(2,128)(2,1)}), bf16[256,2,640]{2,1,0:T(2,128)(2,1)S(1)}, u32[]{:S(2)}, u32[]{:S(2)}) async-start(bf16[256,2,640]{2,1,0:T(2,128)(2,1)} %copy.9), calls=%async_computation | async-start | bytes 1310720 | tf_op jit(solution)/shard_map/all_to_all | solution.py:273
  47.8 30.4 %collective-permute-start = (bf16[616,128]{1,0:T(8,128)(2,1)}, bf16[616,128]{1,0:T(8,128)(2,1)S(1)}, u32[]{:S(2)}, u32[]{:S(2)}) collective-permute-start(bf16[616,128]{1,0:T(8,128)(2,1)} %get-tuple-element.10), channel_id=1, source_target_pairs={{0,4},{4,8},{8,12},{12,16},{16,20},{20,24},{24,28},{28,32},{32,36}... | collective-permute-start | bytes 473096 | tf_op jit(solution)/shard_map/ppermute | solution.py:298
  50.3 28.0 %collective-permute-start.1 = (bf16[616,128]{1,0:T(8,128)(2,1)}, bf16[616,128]{1,0:T(8,128)(2,1)S(1)}, u32[]{:S(2)}, u32[]{:S(2)}) collective-permute-start(bf16[616,128]{1,0:T(8,128)(2,1)} %get-tuple-element.11), channel_id=1, source_target_pairs={{4,0},{8,4},{12,8},{16,12},{20,16},{24,20},{28,24},{32,28},{36,32}... | collective-permute-start | bytes 473096 | tf_op jit(solution)/shard_map/ppermute | solution.py:299
  78.3 0.7 copy-start.6
  78.3 0.7 copy-start.7
  85.3 34.3 %copy-start.2 = (s32[1,256,4]{1,2,0:T(4,128)S(1)}, s32[1,256,4]{1,2,0:T(4,128)}, u32[]{:S(2)}) copy-start(s32[1,256,4]{1,2,0:T(4,128)} %param.11) | copy-start | bytes 12292

commit v4 on v3

--- a/solution.py
+++ b/solution.py
@@ -15,8 +15,8 @@
 SMEM = pl.BlockSpec(memory_space=pltpu.SMEM)
 HBM = pl.BlockSpec(memory_space=pltpu.HBM)
 MIB = 1024 * 1024
-LIMITS = (16, 60, 60, 60, 16)
-GROUP = 4
+LIMITS = (16, 48, 46, 16, 16)
+GROUP = 8
 MAIN, TAIL_AT, TAIL_STEP, WIRE = 256, 512, 64, 640
 
 
@@ -69,15 +69,6 @@
     for r in range(2):
         blocks = [mm(cols[...], hot[:, c * n : (c + 1) * n]) for c in (2 * r, 2 * r + 1)]
         pack_wire(wire, r, blocks, prof)
-
-
-def hot_kernel(slot, hot):
-    width = 512
-
-    @pl.loop(0, hot.shape[1] // width)
-    def _(j):
-        at = pl.multiple_of(j * width, width)
-        write_hot(hot, at, slot[:, pl.ds(at, width)])
 
 
 def edge_kernel(wire, slot, valid, dep, jac_t, arrived, first, last, deps, hot, sems):
@@ -99,7 +90,7 @@
         out[...] = jnp.where(valid[:, at : at + n_pos] > 0, res, 0.0).astype(BF)
 
 
-def main_kernel(rf, inner, arrived_in, hot_in, valid, dep, jac_in, prec_in, part_out, edges_out, *scratch):
+def main_kernel(rf, inner, arrived_in, slot, valid, dep, jac_in, prec_in, part_out, edges_out, *scratch):
     arrived, jac_t, prec, deps, hot, obs_s, res_s, w_s, sc_s, part, in_sem, group_sem, out_sem = scratch
     n_slots = arrived.shape[1]
     n_lines, n_chan, n_pos = dep.shape
@@ -108,13 +99,9 @@
     width = size * n_pos
     count = n_lines // size
 
-    def hot_copy(g):
-        lanes = pl.ds(pl.multiple_of(g * width, width), width)
-        return pltpu.make_async_copy(hot_in.at[:, lanes], hot.at[:, lanes], group_sem.at[0, g])
-
     def dep_copy(g):
         span = pl.ds(g * size, size)
-        return pltpu.make_async_copy(dep.at[span], deps.at[span], group_sem.at[1, g])
+        return pltpu.make_async_copy(dep.at[span], deps.at[span], group_sem.at[g])
 
     whole = [
         pltpu.make_async_copy(src, dst, in_sem.at[k])
@@ -122,17 +109,21 @@
     ]
     for copy in whole:
         copy.start()
-    for g in range(count):
-        hot_copy(g).start()
-        dep_copy(g).start()
+    dep_copy(0).start()
     for copy in whole:
         copy.wait()
 
     @pl.loop(0, count)
     def _(g):
-        hot_copy(g).wait()
         dep_copy(g).wait()
-        lanes = pl.ds(pl.multiple_of(g * width, width), width)
+
+        @pl.when(g + 1 < count)
+        def _():
+            dep_copy(g + 1).start()
+
+        at = pl.multiple_of(g * width, width)
+        lanes = pl.ds(at, width)
+        write_hot(hot, at, slot[:, lanes])
         obs_s[...] = mm(arrived[...], hot[:, lanes]).astype(BF)
         model = mm(jac_t[...], obs_s[...])
         own = jnp.concatenate([deps[g * size + k] for k in range(size)], axis=1)
@@ -179,21 +170,13 @@
         part_copy(q).wait()
 
 
-def finish_kernel(rf, norm, inner, n_band, band, before, after, edges_in, slot, part_in, jac, prec, wire, *scratch):
-    edges, part, sems = scratch
+def finish_kernel(rf, norm, inner, n_band, band, before, after, edges, slot, part, jac, prec, wire):
     prof = jac.shape[0]
     n_slots = part.shape[1]
     n_pos = before.shape[1]
     total = slot.shape[1]
     step = n_slots // 4
-    copies = [pltpu.make_async_copy(edges_in, edges, sems.at[4])]
-    for c in range(4):
-        lanes = pl.ds(c * step, step)
-        copies.append(pltpu.make_async_copy(part_in.at[:, lanes], part.at[:, lanes], sems.at[c]))
-    for copy in copies:
-        copy.start()
     outer = rf * mm(prec[...], jnp.concatenate([before[...], after[...]], axis=1))
-    copies[0].wait()
     ends = []
     for side, bound in ((0, 0), (1, n_band - 1)):
         own = edges[:, 3 * side * n_pos : (3 * side + 1) * n_pos]
@@ -203,8 +186,6 @@
         ends.append((ratio * own - (inside + beyond)).astype(BF))
     scaled = jnp.concatenate(ends, axis=1)
     idx = jnp.concatenate([slot[:, 0:n_pos], slot[:, total - n_pos :]], axis=1)
-    for copy in copies[1:]:
-        copy.wait()
     for r in range(2):
         blocks = []
         for c in (2 * r, 2 * r + 1):
@@ -284,7 +265,6 @@
         scratch=[vm((n_cols, n_slots), BF), vm((prof, n_cols), BF), dma],
     )(columns.T, plan)
     got = exchange(wire)
-    (hot,) = call(hot_kernel, [sds((n_slots, total), BF)], [VMEM], 60, 2**32)(slots)
     line_shape = sds((n_chan, n_pos), BF)
     arrived, first, last = call(
         edge_kernel,
@@ -300,7 +280,7 @@
     part, edges = call(
         functools.partial(main_kernel, rf, inner),
         [sds((n_chan, n_slots), F32), sds((n_chan, 4 * n_pos), F32)],
-        [HBM, HBM, VMEM, HBM, HBM, HBM],
+        [HBM, VMEM, VMEM, HBM, HBM, HBM],
         LIMITS[2],
         2**34,
         scratch=[
@@ -315,19 +295,18 @@
             vm((n_chan, total), BF),
             vm((n_chan, n_slots), F32),
             dma((3,)),
-            dma((2, n_lines // GROUP)),
+            dma((n_lines // GROUP,)),
             dma((6,)),
         ],
         out_specs=[HBM] * 2,
-    )(arrived, hot, valid, dep, jac_t, chan_precision)
+    )(arrived, slots, valid, dep, jac_t, chan_precision)
     band = lax.axis_index("band").reshape(1)
     (wire,) = call(
         functools.partial(finish_kernel, rf, norm, inner, n_band),
         [wire_shape],
-        [SMEM, VMEM, VMEM, HBM, VMEM, HBM, VMEM, VMEM],
+        [SMEM] + [VMEM] * 7,
         LIMITS[3],
         2**31,
-        scratch=[vm((n_chan, 4 * n_pos), F32), vm((n_chan, n_slots), F32), dma((5,))],
     )(band, before, after, edges, slots, part, jacobian, chan_precision)
     back = exchange(wire)
     (grad,) = call(

time: 122 us -> 108 us (0.89)
  Pallas kernels: 44.7 us -> 27.9 us
  waiting for transfers between devices: 15.3 us -> 22.1 us
  local copies, waits for them, and re-layouts: 7.92 us -> 4.56 us
    all_to_all x1, waiting for transfers between devices: 15.3 us -> 22.1 us  [exchange(): lax.all_to_all(sent, ('band', 'lev'), split_axis=0, concat_axis=0, tiled=...]
    pallas_call x1, Pallas kernels: 26.1 us -> 19.4 us  [on_device(): call(functools.partial(main_kernel, rf, inner), [sds((n_chan, n_slots), F...]
    pallas_call x1 -> x0, Pallas kernels: 4.94 us -> none  [on_device(): call(hot_kernel, [sds((n_slots, total), BF)], [VMEM], 60, 2 ** 32)(slots)]
    pallas_call x1, Pallas kernels: 6.34 us -> 2.48 us  [on_device(): call(functools.partial(finish_kernel, rf, norm, inner, n_band), [wire_sha...]
    unnamed x17 -> x15, local copies, waits for them, and re-layouts: 3.65 us -> 2.23 us
    pallas_call x1, Pallas kernels: 3.16 us -> 1.82 us  [on_device(): call(edge_kernel, [sds((prof, n_slots), BF), line_shape, line_shape], [VM...]
  transfers between devices with their start and end apart: 3 -> 3, of which waited for: 1 -> 1; matrix products, arithmetic and copies ran while one was open for 2% -> 0% of each run, Pallas kernels for 25% -> 18%
where the time goes in v4:
time: 108 us; the launch traced here: 107 us
  blocking collectives  32.4 us (30%)
  Pallas kernels  27.9 us (26%)
  waiting for transfers between devices  22.1 us (20%)
  starting transfers between devices  20 us (19%)
  local copies, waits for them, and re-layouts  4.56 us (4%)
    all_to_all x1, blocking collectives, exchange(): lax.all_to_all(sent, ('band', 'lev'), split_axis=0, concat_axis=0, tiled=...  32.4 us
    all_to_all x1, waiting for transfers between devices, exchange(): lax.all_to_all(sent, ('band', 'lev'), split_axis=0, concat_axis=0, tiled=...  22.1 us
    pallas_call x1, Pallas kernels, on_device(): call(functools.partial(main_kernel, rf, inner), [sds((n_chan, n_slots), F...  19.4 us
    all_to_all x1, starting transfers between devices, exchange(): lax.all_to_all(sent, ('band', 'lev'), split_axis=0, concat_axis=0, tiled=...  15.6 us
    pallas_call x1, Pallas kernels, on_device(): call(functools.partial(finish_kernel, rf, norm, inner, n_band), [wire_sha...  2.48 us
    ppermute x1, starting transfers between devices, on_device(): before = lax.ppermute(last, 'band', [(i, i + 1) for i in range(ends)])  2.41 us
    pallas_call x1, Pallas kernels, on_device(): call(collect_kernel, [sds((prof, n_cols), F32)], [VMEM, VMEM], LIMITS[4],...  2.29 us
    unnamed x15, local copies, waits for them, and re-layouts  2.23 us
  transfers between devices with their start and end apart: 3, of which 1 were waited for; matrix products, arithmetic and copies ran while one was open for 0% of the time, Pallas kernels for 18%

profile of v4, /device:TPU:1, one launch (start us, length us, event | category | flops | bytes accessed | tf_op | source)
XLA Modules:
  0.0 107.4 jit_solution(12042877134715090687)
XLA Ops:
  0.0 1.3 %copy-done.1 = bf16[2048,274]{0,1:T(8,128)(2,1)S(1)} copy-done((bf16[2048,274]{0,1:T(8,128)(2,1)S(1)}, bf16[2048,274]{0,1:T(8,128)(2,1)}, u32[]{:S(2)}) %copy-start.1) | copy-done | bytes 1122328
  1.3 0.7 copy-done.3
  1.9 1.9 %shard_map.73 = bf16[2,256,640]{2,1,0:T(8,128)(2,1)S(1)} custom-call(bf16[274,2048]{1,0:T(8,128)(2,1)S(1)} %bitcast.32, s32[4,256]{1,0:T(4,128)S(1)} %bitcast.33), custom_call_target="tpu_custom_call" | custom-call | flops 2147483648 | bytes 8388608 | tf_op jit(solution)/shard_map/pallas_call | solution.py:259
  3.9 0.0 copy-start.6
  3.9 0.0 copy-start
  3.9 0.0 copy-start.5
  3.9 1.5 %copy.9 = bf16[256,2,640]{2,1,0:T(2,128)(2,1)} copy(bf16[256,2,640]{2,0,1:T(8,128)(2,1)S(1)} %bitcast.31) | data formatting | bytes 1310720 | tf_op jit(solution)/shard_map/transpose | solution.py:253
  5.5 15.6 %all-to-all-start = ((bf16[256,2,640]{2,1,0:T(2,128)(2,1)}), bf16[256,2,640]{2,1,0:T(2,128)(2,1)S(1)}, u32[]{:S(2)}, u32[]{:S(2)}) async-start(bf16[256,2,640]{2,1,0:T(2,128)(2,1)} %copy.9), calls=%async_computation | async-start | bytes 1310720 | tf_op jit(solution)/shard_map/all_to_all | solution.py:254
  21.1 0.1 fusion.2
  21.2 0.3 copy.11
  21.5 0.1 bitcast_select_fusion.slot
  21.6 22.1 %all-to-all-done = bf16[256,2,640]{2,1,0:T(2,128)(2,1)S(1)} async-done(((bf16[256,2,640]{2,1,0:T(2,128)(2,1)}), bf16[256,2,640]{2,1,0:T(2,128)(2,1)S(1)}, u32[]{:S(2)}, u32[]{:S(2)}) %all-to-all-start) | async-done | bytes 655392 | tf_op jit(solution)/shard_map/all_to_all | solution.py:254
  43.8 0.1 copy.20
  43.8 0.0 copy-start.2
  43.8 1.8 %shard_map.74 = (bf16[274,1024]{1,0:T(8,128)(2,1)S(1)}, bf16[616,128]{1,0:T(8,128)(2,1)S(1)}, bf16[616,128]{1,0:T(8,128)(2,1)S(1)}) custom-call(bf16[2,256,640]{2,1,0:T(8,128)(2,1)S(1)} %bitcast.26, s32[1,4096]{1,0:T(1,128)S(1)} %bitcast_select_fusion.slot, s32[1,4096]{1,0:T(1,128)S(1)} %bitcast_convert_fusion.valid, bf16[32,616,128]{2,1,0:T(8,128)(2,1)} %bitcast.35, ...), custom_call_target="tpu_custom_call" | custom-call | flops 1073741824 | bytes 8388608 | tf_op jit(solution)/shard_map/pallas_call | solution.py:269
  45.7 2.4 %collective-permute-start = (bf16[616,128]{1,0:T(8,128)(2,1)S(1)}, bf16[616,128]{1,0:T(8,128)(2,1)S(1)}, u32[]{:S(2)}, u32[]{:S(2)}) collective-permute-start(bf16[616,128]{1,0:T(8,128)(2,1)S(1)} %get-tuple-element.10), channel_id=1, source_target_pairs={{0,4},{4,8},{8,12},{12,16},{16,20},{20,24},{24,28},{28,32},{32,36}... | collective-permute-start | bytes 473096 | tf_op jit(solution)/shard_map/ppermute | solution.py:278
  48.1 1.9 %collective-permute-start.1 = (bf16[616,128]{1,0:T(8,128)(2,1)S(1)}, bf16[616,128]{1,0:T(8,128)(2,1)S(1)}, u32[]{:S(2)}, u32[]{:S(2)}) collective-permute-start(bf16[616,128]{1,0:T(8,128)(2,1)S(1)} %get-tuple-element.11), channel_id=1, source_target_pairs={{4,0},{8,4},{12,8},{16,12},{20,16},{24,20},{28,24},{32,28},{36,32}... | collective-permute-start | bytes 473096 | tf_op jit(solution)/shard_map/ppermute | solution.py:279
  50.0 19.4 %shard_map.75 = (f32[616,1024]{1,0:T(8,128)S(1)}, f32[616,512]{1,0:T(8,128)S(1)}) custom-call(bf16[274,1024]{1,0:T(8,128)(2,1)S(1)} %get-tuple-element.12.arrived_in, s32[1,4096]{1,0:T(1,128)S(1)} %bitcast_select_fusion.slot, s32[1,4096]{1,0:T(1,128)S(1)} %bitcast_convert_fusion.valid, bf16[32,616,128]{2,1,0:T(8,128)(2,1)} %bitcast.36, ...), custom_call_target="tpu_custom_call" | custom-call | flops 17179869184 | bytes 8388608 | tf_op jit(solution)/shard_map/pallas_call | solution.py:280
  69.4 2.5 %shard_map.76 = bf16[2,256,640]{2,1,0:T(8,128)(2,1)S(1)} custom-call(s32[1]{0:T(128)} %bitcast.band, bf16[616,128]{1,0:T(8,128)(2,1)S(1)} %collective-permute-done.before, bf16[616,128]{1,0:T(8,128)(2,1)S(1)} %collective-permute-done.1.after, f32[616,512]{1,0:T(8,128)S(1)} %get-tuple-element.13.edges, s32[1,4096]{1,0:T(1,128)S(1)} %bitcast_select_fusion.slot, ...), custom_call_target="tpu_custom_call" | custom-call | flops 2147483648 | bytes 8388608 | tf_op jit(solution)/shard_map/pallas_call | solution.py:304
  71.9 0.0 copy-start.4
  71.9 0.7 copy.12
  72.6 32.4 %all_to_all.10 = bf16[256,2,640]{2,1,0:T(2,128)(2,1)S(1)} all-to-all(bf16[256,2,640]{2,1,0:T(2,128)(2,1)S(1)} %copy.12), channel_id=1, replica_groups=mesh['band'=64,'lev'=4] {'band','lev'}, dimensions={0} | all-to-all | bytes 1310720 | tf_op jit(solution)/shard_map/all_to_all | solution.py:254
  105.1 0.1 copy.19
  105.1 2.3 %shard_map.77 = f32[274,2048]{1,0:T(8,128)} custom-call(bf16[2,256,640]{2,1,0:T(8,128)(2,1)S(1)} %bitcast.30, s32[4,256]{1,0:T(4,128)S(1)} %bitcast.34), custom_call_target="tpu_custom_call" | custom-call | flops 2147483648 | bytes 8388608 | tf_op jit(solution)/shard_map/pallas_call | solution.py:312
  (10 shorter events, 0.0 us)
Async XLA Ops:
  0.0 1.3 %copy-start.1 = (bf16[2048,274]{0,1:T(8,128)(2,1)S(1)}, bf16[2048,274]{0,1:T(8,128)(2,1)}, u32[]{:S(2)}) copy-start(bf16[2048,274]{0,1:T(8,128)(2,1)} %param.7) | copy-start | bytes 3366916
  1.3 0.7 copy-start.3
  3.9 17.2 %copy-start.6 = (s32[1,32]{1,0:T(1,128)S(1)}, s32[1,32]{1,0:T(1,128)}, u32[]{:S(2)}) copy-start(s32[1,32]{1,0:T(1,128)} %param.13) | copy-start | bytes 388
  3.9 17.3 %copy-start = (bf16[274,616]{1,0:T(8,128)(2,1)S(1)}, bf16[274,616]{1,0:T(8,128)(2,1)}, u32[]{:S(2)}) copy-start(bf16[274,616]{1,0:T(8,128)(2,1)} %jac.1) | copy-start | bytes 1012708
  3.9 17.6 %copy-start.5 = (s32[1,32,128]{2,1,0:T(8,128)S(1)}, s32[1,32,128]{2,1,0:T(8,128)}, u32[]{:S(2)}) copy-start(s32[1,32,128]{2,1,0:T(8,128)} %param.12) | copy-start | bytes 49156
  5.5 38.3 %all-to-all-start = ((bf16[256,2,640]{2,1,0:T(2,128)(2,1)}), bf16[256,2,640]{2,1,0:T(2,128)(2,1)S(1)}, u32[]{:S(2)}, u32[]{:S(2)}) async-start(bf16[256,2,640]{2,1,0:T(2,128)(2,1)} %copy.9), calls=%async_computation | async-start | bytes 1310720 | tf_op jit(solution)/shard_map/all_to_all | solution.py:254
  43.8 6.2 %copy-start.2 = (bf16[616,616]{1,0:T(8,128)(2,1)S(1)}, bf16[616,616]{1,0:T(8,128)(2,1)}, u32[]{:S(2)}) copy-start(bf16[616,616]{1,0:T(8,128)(2,1)} %prec.1) | copy-start | bytes 2276740
  45.7 23.7 %collective-permute-start = (bf16[616,128]{1,0:T(8,128)(2,1)S(1)}, bf16[616,128]{1,0:T(8,128)(2,1)S(1)}, u32[]{:S(2)}, u32[]{:S(2)}) collective-permute-start(bf16[616,128]{1,0:T(8,128)(2,1)S(1)} %get-tuple-element.10), channel_id=1, source_target_pairs={{0,4},{4,8},{8,12},{12,16},{16,20},{20,24},{24,28},{28,32},{32,36}... | collective-permute-start | bytes 473096 | tf_op jit(solution)/shard_map/ppermute | solution.py:278
  48.1 21.3 %collective-permute-start.1 = (bf16[616,128]{1,0:T(8,128)(2,1)S(1)}, bf16[616,128]{1,0:T(8,128)(2,1)S(1)}, u32[]{:S(2)}, u32[]{:S(2)}) collective-permute-start(bf16[616,128]{1,0:T(8,128)(2,1)S(1)} %get-tuple-element.11), channel_id=1, source_target_pairs={{4,0},{8,4},{12,8},{16,12},{20,16},{24,20},{28,24},{32,28},{36,32}... | collective-permute-start | bytes 473096 | tf_op jit(solution)/shard_map/ppermute | solution.py:279
  71.9 33.2 %copy-start.4 = (s32[1,256,4]{1,2,0:T(4,128)S(1)}, s32[1,256,4]{1,2,0:T(4,128)}, u32[]{:S(2)}) copy-start(s32[1,256,4]{1,2,0:T(4,128)} %param.11) | copy-start | bytes 12292

commit v5 on v4

--- a/solution.py
+++ b/solution.py
@@ -15,7 +15,7 @@
 SMEM = pl.BlockSpec(memory_space=pltpu.SMEM)
 HBM = pl.BlockSpec(memory_space=pltpu.HBM)
 MIB = 1024 * 1024
-LIMITS = (16, 48, 46, 16, 16)
+LIMITS = (53, 48, 46, 16, 16)
 GROUP = 8
 MAIN, TAIL_AT, TAIL_STEP, WIRE = 256, 512, 64, 640
 

time: 108 us -> 107 us (level)
  local copies, waits for them, and re-layouts: 4.56 us -> 3.31 us
    unnamed x15 -> x13, local copies, waits for them, and re-layouts: 2.23 us -> 0.97 us
where the time goes in v5:
time: 107 us
  blocking collectives  32.5 us (30%)
  Pallas kernels  28.7 us (27%)
  waiting for transfers between devices  22.1 us (21%)
  starting transfers between devices  20 us (19%)
  local copies, waits for them, and re-layouts  3.31 us (3%)
    all_to_all x1, blocking collectives, exchange(): lax.all_to_all(sent, ('band', 'lev'), split_axis=0, concat_axis=0, tiled=...  32.5 us
    all_to_all x1, waiting for transfers between devices, exchange(): lax.all_to_all(sent, ('band', 'lev'), split_axis=0, concat_axis=0, tiled=...  22.1 us
    pallas_call x1, Pallas kernels, on_device(): call(functools.partial(main_kernel, rf, inner), [sds((n_chan, n_slots), F...  19.4 us
    all_to_all x1, starting transfers between devices, exchange(): lax.all_to_all(sent, ('band', 'lev'), split_axis=0, concat_axis=0, tiled=...  15.6 us
    pallas_call x1, Pallas kernels, on_device(): call(send_kernel, [wire_shape], [HBM, VMEM], LIMITS[0], 2 ** 31, scratch=...  2.75 us
    pallas_call x1, Pallas kernels, on_device(): call(functools.partial(finish_kernel, rf, norm, inner, n_band), [wire_sha...  2.48 us
    ppermute x1, starting transfers between devices, on_device(): before = lax.ppermute(last, 'band', [(i, i + 1) for i in range(ends)])  2.41 us
    pallas_call x1, Pallas kernels, on_device(): call(collect_kernel, [sds((prof, n_cols), F32)], [VMEM, VMEM], LIMITS[4],...  2.29 us
  transfers between devices with their start and end apart: 3, of which 1 were waited for; matrix products, arithmetic and copies ran while one was open for 0% of the time, Pallas kernels for 18%

profile of v5, /device:TPU:1, one launch (start us, length us, event | category | flops | bytes accessed | tf_op | source)
XLA Modules:
  0.0 107.0 jit_solution(6470635666850317579)
XLA Ops:
  0.0 0.7 copy-done.2
  0.7 2.7 %shard_map.73 = bf16[2,256,640]{2,1,0:T(8,128)(2,1)S(1)} custom-call(bf16[274,2048]{1,0:T(8,128)(2,1)} %bitcast.38, s32[4,256]{1,0:T(4,128)S(1)} %bitcast.32), custom_call_target="tpu_custom_call" | custom-call | flops 2147483648 | bytes 8388608 | tf_op jit(solution)/shard_map/pallas_call | solution.py:259
  3.4 0.0 copy-start.5
  3.5 0.0 copy-start
  3.5 0.0 copy-start.4
  3.5 1.5 %copy.9 = bf16[256,2,640]{2,1,0:T(2,128)(2,1)} copy(bf16[256,2,640]{2,0,1:T(8,128)(2,1)S(1)} %bitcast.31) | data formatting | bytes 1310720 | tf_op jit(solution)/shard_map/transpose | solution.py:253
  5.0 15.6 %all-to-all-start = ((bf16[256,2,640]{2,1,0:T(2,128)(2,1)}), bf16[256,2,640]{2,1,0:T(2,128)(2,1)S(1)}, u32[]{:S(2)}, u32[]{:S(2)}) async-start(bf16[256,2,640]{2,1,0:T(2,128)(2,1)} %copy.9), calls=%async_computation | async-start | bytes 1310720 | tf_op jit(solution)/shard_map/all_to_all | solution.py:254
  20.7 0.1 fusion.2
  20.8 0.3 copy.11
  21.0 0.1 bitcast_select_fusion.slot
  21.2 22.1 %all-to-all-done = bf16[256,2,640]{2,1,0:T(2,128)(2,1)S(1)} async-done(((bf16[256,2,640]{2,1,0:T(2,128)(2,1)}), bf16[256,2,640]{2,1,0:T(2,128)(2,1)S(1)}, u32[]{:S(2)}, u32[]{:S(2)}) %all-to-all-start) | async-done | bytes 655392 | tf_op jit(solution)/shard_map/all_to_all | solution.py:254
  43.3 0.1 copy.20
  43.4 0.0 copy-start.1
  43.4 1.8 %shard_map.74 = (bf16[274,1024]{1,0:T(8,128)(2,1)S(1)}, bf16[616,128]{1,0:T(8,128)(2,1)S(1)}, bf16[616,128]{1,0:T(8,128)(2,1)S(1)}) custom-call(bf16[2,256,640]{2,1,0:T(8,128)(2,1)S(1)} %bitcast.26, s32[1,4096]{1,0:T(1,128)S(1)} %bitcast_select_fusion.slot, s32[1,4096]{1,0:T(1,128)S(1)} %bitcast_convert_fusion.valid, bf16[32,616,128]{2,1,0:T(8,128)(2,1)} %bitcast.34, ...), custom_call_target="tpu_custom_call" | custom-call | flops 1073741824 | bytes 8388608 | tf_op jit(solution)/shard_map/pallas_call | solution.py:269
  45.2 2.4 %collective-permute-start = (bf16[616,128]{1,0:T(8,128)(2,1)S(1)}, bf16[616,128]{1,0:T(8,128)(2,1)S(1)}, u32[]{:S(2)}, u32[]{:S(2)}) collective-permute-start(bf16[616,128]{1,0:T(8,128)(2,1)S(1)} %get-tuple-element.10), channel_id=1, source_target_pairs={{0,4},{4,8},{8,12},{12,16},{16,20},{20,24},{24,28},{28,32},{32,36}... | collective-permute-start | bytes 473096 | tf_op jit(solution)/shard_map/ppermute | solution.py:278
  47.6 1.9 %collective-permute-start.1 = (bf16[616,128]{1,0:T(8,128)(2,1)S(1)}, bf16[616,128]{1,0:T(8,128)(2,1)S(1)}, u32[]{:S(2)}, u32[]{:S(2)}) collective-permute-start(bf16[616,128]{1,0:T(8,128)(2,1)S(1)} %get-tuple-element.11), channel_id=1, source_target_pairs={{4,0},{8,4},{12,8},{16,12},{20,16},{24,20},{28,24},{32,28},{36,32}... | collective-permute-start | bytes 473096 | tf_op jit(solution)/shard_map/ppermute | solution.py:279
  49.6 19.4 %shard_map.75 = (f32[616,1024]{1,0:T(8,128)S(1)}, f32[616,512]{1,0:T(8,128)S(1)}) custom-call(bf16[274,1024]{1,0:T(8,128)(2,1)S(1)} %get-tuple-element.12.arrived_in, s32[1,4096]{1,0:T(1,128)S(1)} %bitcast_select_fusion.slot, s32[1,4096]{1,0:T(1,128)S(1)} %bitcast_convert_fusion.valid, bf16[32,616,128]{2,1,0:T(8,128)(2,1)} %bitcast.35, ...), custom_call_target="tpu_custom_call" | custom-call | flops 17179869184 | bytes 8388608 | tf_op jit(solution)/shard_map/pallas_call | solution.py:280
  68.9 0.0 collective-permute-done.before
  69.0 2.5 %shard_map.76 = bf16[2,256,640]{2,1,0:T(8,128)(2,1)S(1)} custom-call(s32[1]{0:T(128)} %bitcast.band, bf16[616,128]{1,0:T(8,128)(2,1)S(1)} %collective-permute-done.before, bf16[616,128]{1,0:T(8,128)(2,1)S(1)} %collective-permute-done.1.after, f32[616,512]{1,0:T(8,128)S(1)} %get-tuple-element.13.edges, s32[1,4096]{1,0:T(1,128)S(1)} %bitcast_select_fusion.slot, ...), custom_call_target="tpu_custom_call" | custom-call | flops 2147483648 | bytes 8388608 | tf_op jit(solution)/shard_map/pallas_call | solution.py:304
  71.4 0.0 copy-start.3
  71.5 0.7 copy.12
  72.1 32.5 %all_to_all.10 = bf16[256,2,640]{2,1,0:T(2,128)(2,1)S(1)} all-to-all(bf16[256,2,640]{2,1,0:T(2,128)(2,1)S(1)} %copy.12), channel_id=1, replica_groups=mesh['band'=64,'lev'=4] {'band','lev'}, dimensions={0} | all-to-all | bytes 1310720 | tf_op jit(solution)/shard_map/all_to_all | solution.py:254
  104.6 0.1 copy.19
  104.7 2.3 %shard_map.77 = f32[274,2048]{1,0:T(8,128)} custom-call(bf16[2,256,640]{2,1,0:T(8,128)(2,1)S(1)} %bitcast.30, s32[4,256]{1,0:T(4,128)S(1)} %bitcast.33), custom_call_target="tpu_custom_call" | custom-call | flops 2147483648 | bytes 8388608 | tf_op jit(solution)/shard_map/pallas_call | solution.py:312
  (8 shorter events, 0.0 us)
Async XLA Ops:
  0.0 0.7 copy-start.2
  3.4 17.2 %copy-start.5 = (s32[1,32]{1,0:T(1,128)S(1)}, s32[1,32]{1,0:T(1,128)}, u32[]{:S(2)}) copy-start(s32[1,32]{1,0:T(1,128)} %param.13) | copy-start | bytes 388
  3.5 17.3 %copy-start = (bf16[274,616]{1,0:T(8,128)(2,1)S(1)}, bf16[274,616]{1,0:T(8,128)(2,1)}, u32[]{:S(2)}) copy-start(bf16[274,616]{1,0:T(8,128)(2,1)} %jac.1) | copy-start | bytes 1012708
  3.5 17.6 %copy-start.4 = (s32[1,32,128]{2,1,0:T(8,128)S(1)}, s32[1,32,128]{2,1,0:T(8,128)}, u32[]{:S(2)}) copy-start(s32[1,32,128]{2,1,0:T(8,128)} %param.12) | copy-start | bytes 49156
  5.0 38.3 %all-to-all-start = ((bf16[256,2,640]{2,1,0:T(2,128)(2,1)}), bf16[256,2,640]{2,1,0:T(2,128)(2,1)S(1)}, u32[]{:S(2)}, u32[]{:S(2)}) async-start(bf16[256,2,640]{2,1,0:T(2,128)(2,1)} %copy.9), calls=%async_computation | async-start | bytes 1310720 | tf_op jit(solution)/shard_map/all_to_all | solution.py:254
  43.4 6.2 %copy-start.1 = (bf16[616,616]{1,0:T(8,128)(2,1)S(1)}, bf16[616,616]{1,0:T(8,128)(2,1)}, u32[]{:S(2)}) copy-start(bf16[616,616]{1,0:T(8,128)(2,1)} %prec.1) | copy-start | bytes 2276740
  45.2 23.7 %collective-permute-start = (bf16[616,128]{1,0:T(8,128)(2,1)S(1)}, bf16[616,128]{1,0:T(8,128)(2,1)S(1)}, u32[]{:S(2)}, u32[]{:S(2)}) collective-permute-start(bf16[616,128]{1,0:T(8,128)(2,1)S(1)} %get-tuple-element.10), channel_id=1, source_target_pairs={{0,4},{4,8},{8,12},{12,16},{16,20},{20,24},{24,28},{28,32},{32,36}... | collective-permute-start | bytes 473096 | tf_op jit(solution)/shard_map/ppermute | solution.py:278
  47.6 21.3 %collective-permute-start.1 = (bf16[616,128]{1,0:T(8,128)(2,1)S(1)}, bf16[616,128]{1,0:T(8,128)(2,1)S(1)}, u32[]{:S(2)}, u32[]{:S(2)}) collective-permute-start(bf16[616,128]{1,0:T(8,128)(2,1)S(1)} %get-tuple-element.11), channel_id=1, source_target_pairs={{4,0},{8,4},{12,8},{16,12},{20,16},{24,20},{28,24},{32,28},{36,32}... | collective-permute-start | bytes 473096 | tf_op jit(solution)/shard_map/ppermute | solution.py:279
  71.4 33.2 %copy-start.3 = (s32[1,256,4]{1,2,0:T(4,128)S(1)}, s32[1,256,4]{1,2,0:T(4,128)}, u32[]{:S(2)}) copy-start(s32[1,256,4]{1,2,0:T(4,128)} %param.11) | copy-start | bytes 12292

commit v6 on v5

--- a/solution.py
+++ b/solution.py
@@ -63,9 +63,11 @@
     copy = pltpu.make_async_copy(cols_in, cols, sem)
     copy.start()
     n = plan.shape[1]
-    for c in range(4):
+    for c in range(2):
         write_hot(hot, c * n, plan[c : c + 1, :])
     copy.wait()
+    for c in range(2, 4):
+        write_hot(hot, c * n, plan[c : c + 1, :])
     for r in range(2):
         blocks = [mm(cols[...], hot[:, c * n : (c + 1) * n]) for c in (2 * r, 2 * r + 1)]
         pack_wire(wire, r, blocks, prof)
@@ -144,21 +146,22 @@
             sc_s[rows, i * n_pos : (i + 1) * n_pos] = ((inner / rf) * here - (before + after)).astype(BF)
             before, here = here, after
 
-    @pl.loop(0, n_chan // 16)
+    @pl.loop(0, n_chan // 32)
     def _(c):
-        scale(pl.ds(pl.multiple_of(c * 16, 16), 16))
-
-    if n_chan % 16:
-        scale(pl.ds(n_chan // 16 * 16, n_chan % 16))
+        scale(pl.ds(pl.multiple_of(c * 32, 32), 16))
+        scale(pl.ds(pl.multiple_of(c * 32 + 16, 16), 16))
+
+    for at in range(n_chan // 32 * 32, n_chan, 16):
+        scale(pl.ds(at, min(16, n_chan - at)))
 
     inside = slice(n_pos, total - n_pos)
-    step = n_slots // 4
+    step = n_slots // 2
 
     def part_copy(q):
         lanes = pl.ds(pl.multiple_of(q * step, step), step)
         return pltpu.make_async_copy(part.at[:, lanes], part_out.at[:, lanes], out_sem.at[q])
 
-    @pl.loop(0, 4)
+    @pl.loop(0, 2)
     def _(q):
         at = pl.multiple_of(q * step, step)
         part[:, pl.ds(at, step)] = mm_nt(sc_s[:, inside], hot[pl.ds(at, step), inside])
@@ -166,7 +169,7 @@
 
     for copy in sides:
         copy.wait()
-    for q in range(4):
+    for q in range(2):
         part_copy(q).wait()
 
 

time: 107 us -> 107 us (level)
  no operation moved by 1% of the time
where the time goes in v6:
time: 107 us
  blocking collectives  32.5 us (30%)
  Pallas kernels  28.1 us (26%)
  waiting for transfers between devices  22.1 us (21%)
  starting transfers between devices  20 us (19%)
  local copies, waits for them, and re-layouts  3.31 us (3%)
    all_to_all x1, blocking collectives, exchange(): lax.all_to_all(sent, ('band', 'lev'), split_axis=0, concat_axis=0, tiled=...  32.5 us
    all_to_all x1, waiting for transfers between devices, exchange(): lax.all_to_all(sent, ('band', 'lev'), split_axis=0, concat_axis=0, tiled=...  22.1 us
    pallas_call x1, Pallas kernels, on_device(): call(functools.partial(main_kernel, rf, inner), [sds((n_chan, n_slots), F...  18.8 us
    all_to_all x1, starting transfers between devices, exchange(): lax.all_to_all(sent, ('band', 'lev'), split_axis=0, concat_axis=0, tiled=...  15.6 us
    pallas_call x1, Pallas kernels, on_device(): call(send_kernel, [wire_shape], [HBM, VMEM], LIMITS[0], 2 ** 31, scratch=...  2.75 us
    pallas_call x1, Pallas kernels, on_device(): call(functools.partial(finish_kernel, rf, norm, inner, n_band), [wire_sha...  2.48 us
    ppermute x1, starting transfers between devices, on_device(): before = lax.ppermute(last, 'band', [(i, i + 1) for i in range(ends)])  2.41 us
    pallas_call x1, Pallas kernels, on_device(): call(collect_kernel, [sds((prof, n_cols), F32)], [VMEM, VMEM], LIMITS[4],...  2.29 us
  transfers between devices with their start and end apart: 3, of which 1 were waited for; matrix products, arithmetic and copies ran while one was open for 0% of the time, Pallas kernels for 18%

profile of v6, /device:TPU:1, one launch (start us, length us, event | category | flops | bytes accessed | tf_op | source)
XLA Modules:
  0.0 106.6 jit_solution(15167637461223812115)
XLA Ops:
  0.0 0.7 copy-done.2
  0.7 2.7 %shard_map.73 = bf16[2,256,640]{2,1,0:T(8,128)(2,1)S(1)} custom-call(bf16[274,2048]{1,0:T(8,128)(2,1)} %bitcast.38, s32[4,256]{1,0:T(4,128)S(1)} %bitcast.32), custom_call_target="tpu_custom_call" | custom-call | flops 2147483648 | bytes 8388608 | tf_op jit(solution)/shard_map/pallas_call | solution.py:262
  3.4 0.0 copy-start.5
  3.5 0.0 copy-start
  3.5 0.0 copy-start.4
  3.5 1.5 %copy.9 = bf16[256,2,640]{2,1,0:T(2,128)(2,1)} copy(bf16[256,2,640]{2,0,1:T(8,128)(2,1)S(1)} %bitcast.31) | data formatting | bytes 1310720 | tf_op jit(solution)/shard_map/transpose | solution.py:256
  5.0 15.6 %all-to-all-start = ((bf16[256,2,640]{2,1,0:T(2,128)(2,1)}), bf16[256,2,640]{2,1,0:T(2,128)(2,1)S(1)}, u32[]{:S(2)}, u32[]{:S(2)}) async-start(bf16[256,2,640]{2,1,0:T(2,128)(2,1)} %copy.9), calls=%async_computation | async-start | bytes 1310720 | tf_op jit(solution)/shard_map/all_to_all | solution.py:257
  20.7 0.1 fusion.2
  20.8 0.3 copy.11
  21.0 0.1 bitcast_select_fusion.slot
  21.2 22.1 %all-to-all-done = bf16[256,2,640]{2,1,0:T(2,128)(2,1)S(1)} async-done(((bf16[256,2,640]{2,1,0:T(2,128)(2,1)}), bf16[256,2,640]{2,1,0:T(2,128)(2,1)S(1)}, u32[]{:S(2)}, u32[]{:S(2)}) %all-to-all-start) | async-done | bytes 655392 | tf_op jit(solution)/shard_map/all_to_all | solution.py:257
  43.3 0.1 copy.20
  43.4 0.0 copy-start.1
  43.4 1.8 %shard_map.74 = (bf16[274,1024]{1,0:T(8,128)(2,1)S(1)}, bf16[616,128]{1,0:T(8,128)(2,1)S(1)}, bf16[616,128]{1,0:T(8,128)(2,1)S(1)}) custom-call(bf16[2,256,640]{2,1,0:T(8,128)(2,1)S(1)} %bitcast.26, s32[1,4096]{1,0:T(1,128)S(1)} %bitcast_select_fusion.slot, s32[1,4096]{1,0:T(1,128)S(1)} %bitcast_convert_fusion.valid, bf16[32,616,128]{2,1,0:T(8,128)(2,1)} %bitcast.34, ...), custom_call_target="tpu_custom_call" | custom-call | flops 1073741824 | bytes 8388608 | tf_op jit(solution)/shard_map/pallas_call | solution.py:272
  45.2 2.4 %collective-permute-start = (bf16[616,128]{1,0:T(8,128)(2,1)S(1)}, bf16[616,128]{1,0:T(8,128)(2,1)S(1)}, u32[]{:S(2)}, u32[]{:S(2)}) collective-permute-start(bf16[616,128]{1,0:T(8,128)(2,1)S(1)} %get-tuple-element.10), channel_id=1, source_target_pairs={{0,4},{4,8},{8,12},{12,16},{16,20},{20,24},{24,28},{28,32},{32,36}... | collective-permute-start | bytes 473096 | tf_op jit(solution)/shard_map/ppermute | solution.py:281
  47.6 1.9 %collective-permute-start.1 = (bf16[616,128]{1,0:T(8,128)(2,1)S(1)}, bf16[616,128]{1,0:T(8,128)(2,1)S(1)}, u32[]{:S(2)}, u32[]{:S(2)}) collective-permute-start(bf16[616,128]{1,0:T(8,128)(2,1)S(1)} %get-tuple-element.11), channel_id=1, source_target_pairs={{4,0},{8,4},{12,8},{16,12},{20,16},{24,20},{28,24},{32,28},{36,32}... | collective-permute-start | bytes 473096 | tf_op jit(solution)/shard_map/ppermute | solution.py:282
  49.6 18.8 %shard_map.75 = (f32[616,1024]{1,0:T(8,128)S(1)}, f32[616,512]{1,0:T(8,128)S(1)}) custom-call(bf16[274,1024]{1,0:T(8,128)(2,1)S(1)} %get-tuple-element.12.arrived_in, s32[1,4096]{1,0:T(1,128)S(1)} %bitcast_select_fusion.slot, s32[1,4096]{1,0:T(1,128)S(1)} %bitcast_convert_fusion.valid, bf16[32,616,128]{2,1,0:T(8,128)(2,1)} %bitcast.35, ...), custom_call_target="tpu_custom_call" | custom-call | flops 17179869184 | bytes 8388608 | tf_op jit(solution)/shard_map/pallas_call | solution.py:283
  68.4 0.0 collective-permute-done.before
  68.4 2.5 %shard_map.76 = bf16[2,256,640]{2,1,0:T(8,128)(2,1)S(1)} custom-call(s32[1]{0:T(128)} %bitcast.band, bf16[616,128]{1,0:T(8,128)(2,1)S(1)} %collective-permute-done.before, bf16[616,128]{1,0:T(8,128)(2,1)S(1)} %collective-permute-done.1.after, f32[616,512]{1,0:T(8,128)S(1)} %get-tuple-element.13.edges, s32[1,4096]{1,0:T(1,128)S(1)} %bitcast_select_fusion.slot, ...), custom_call_target="tpu_custom_call" | custom-call | flops 2147483648 | bytes 8388608 | tf_op jit(solution)/shard_map/pallas_call | solution.py:307
  70.9 0.0 copy-start.3
  70.9 0.7 copy.12
  71.6 32.5 %all_to_all.10 = bf16[256,2,640]{2,1,0:T(2,128)(2,1)S(1)} all-to-all(bf16[256,2,640]{2,1,0:T(2,128)(2,1)S(1)} %copy.12), channel_id=1, replica_groups=mesh['band'=64,'lev'=4] {'band','lev'}, dimensions={0} | all-to-all | bytes 1310720 | tf_op jit(solution)/shard_map/all_to_all | solution.py:257
  104.1 0.1 copy.19
  104.1 2.3 %shard_map.77 = f32[274,2048]{1,0:T(8,128)} custom-call(bf16[2,256,640]{2,1,0:T(8,128)(2,1)S(1)} %bitcast.30, s32[4,256]{1,0:T(4,128)S(1)} %bitcast.33), custom_call_target="tpu_custom_call" | custom-call | flops 2147483648 | bytes 8388608 | tf_op jit(solution)/shard_map/pallas_call | solution.py:315
  (8 shorter events, 0.0 us)
Async XLA Ops:
  0.0 0.7 copy-start.2
  3.4 17.2 %copy-start.5 = (s32[1,32]{1,0:T(1,128)S(1)}, s32[1,32]{1,0:T(1,128)}, u32[]{:S(2)}) copy-start(s32[1,32]{1,0:T(1,128)} %param.13) | copy-start | bytes 388
  3.5 17.3 %copy-start = (bf16[274,616]{1,0:T(8,128)(2,1)S(1)}, bf16[274,616]{1,0:T(8,128)(2,1)}, u32[]{:S(2)}) copy-start(bf16[274,616]{1,0:T(8,128)(2,1)} %jac.1) | copy-start | bytes 1012708
  3.5 17.6 %copy-start.4 = (s32[1,32,128]{2,1,0:T(8,128)S(1)}, s32[1,32,128]{2,1,0:T(8,128)}, u32[]{:S(2)}) copy-start(s32[1,32,128]{2,1,0:T(8,128)} %param.12) | copy-start | bytes 49156
  5.0 38.3 %all-to-all-start = ((bf16[256,2,640]{2,1,0:T(2,128)(2,1)}), bf16[256,2,640]{2,1,0:T(2,128)(2,1)S(1)}, u32[]{:S(2)}, u32[]{:S(2)}) async-start(bf16[256,2,640]{2,1,0:T(2,128)(2,1)} %copy.9), calls=%async_computation | async-start | bytes 1310720 | tf_op jit(solution)/shard_map/all_to_all | solution.py:257
  43.4 6.2 %copy-start.1 = (bf16[616,616]{1,0:T(8,128)(2,1)S(1)}, bf16[616,616]{1,0:T(8,128)(2,1)}, u32[]{:S(2)}) copy-start(bf16[616,616]{1,0:T(8,128)(2,1)} %prec.1) | copy-start | bytes 2276740
  45.2 23.2 %collective-permute-start = (bf16[616,128]{1,0:T(8,128)(2,1)S(1)}, bf16[616,128]{1,0:T(8,128)(2,1)S(1)}, u32[]{:S(2)}, u32[]{:S(2)}) collective-permute-start(bf16[616,128]{1,0:T(8,128)(2,1)S(1)} %get-tuple-element.10), channel_id=1, source_target_pairs={{0,4},{4,8},{8,12},{12,16},{16,20},{20,24},{24,28},{28,32},{32,36}... | collective-permute-start | bytes 473096 | tf_op jit(solution)/shard_map/ppermute | solution.py:281
  47.6 20.8 %collective-permute-start.1 = (bf16[616,128]{1,0:T(8,128)(2,1)S(1)}, bf16[616,128]{1,0:T(8,128)(2,1)S(1)}, u32[]{:S(2)}, u32[]{:S(2)}) collective-permute-start(bf16[616,128]{1,0:T(8,128)(2,1)S(1)} %get-tuple-element.11), channel_id=1, source_target_pairs={{4,0},{8,4},{12,8},{16,12},{20,16},{24,20},{28,24},{32,28},{36,32}... | collective-permute-start | bytes 473096 | tf_op jit(solution)/shard_map/ppermute | solution.py:282
  70.9 33.2 %copy-start.3 = (s32[1,256,4]{1,2,0:T(4,128)S(1)}, s32[1,256,4]{1,2,0:T(4,128)}, u32[]{:S(2)}) copy-start(s32[1,256,4]{1,2,0:T(4,128)} %param.11) | copy-start | bytes 12292
